TPU v7x, 32 devices: a whole 2x2x4 slice. The times are simulated.
32 devices in a mesh: prow: 4 (over y, x), pcol: 8 (over z, core).
Axes of the slice: x: 2, y: 2, z: 4, core: 2. Of those that a mesh axis runs over, the one named last changes fastest.
Arguments:
- diag_block: float32 [128, 128], replicated, may hold values from 0 to 1.03, as said below
- panel: float32 [8192, 128], P(('prow', 'pcol')), may hold values from -0.2 to 1.2
- slab: float32 [8192, 2048], P('prow', 'pcol'), may hold values from -6 to 6
Outputs:
- slab_next: float32 [8192, 2048], P('prow', 'pcol')
- panel_factor: float32 [8192, 128], P(('prow', 'pcol'))
Inputs may be any that keep to these rules, and one draw needn't show every extreme that they name: diag_block is symmetric positive definite.
All inputs are finite; a program needn't handle non-finite values.
Results may differ from a plain program's by a relative error of at most 0.00091.
Values may be sent and summed in bfloat16 or wider, within the bound.
No kernel may reach another device: no remote copies, remote signals or barrier semaphores. Data moves between devices by JAX's collectives and lax.ppermute only.
A program may use at most 64 MiB of HBM per device.

v0:
```python
import functools

import jax
import jax.numpy as jnp
from jax import lax
from jax.experimental import pallas as pl
from jax.experimental.pallas import tpu as pltpu
from jax.sharding import PartitionSpec as P


GROUP = 8
EXACT = lax.Precision.HIGHEST
NT = (((1,), (1,)), ((), ()))


def inverse_factor_kernel(diag_ref, out_ref):
    n = diag_ref.shape[0]
    lane = lax.broadcasted_iota(jnp.int32, (GROUP, n), 1)
    sub = lax.broadcasted_iota(jnp.int32, (GROUP, n), 0)
    rows = [diag_ref[i : i + GROUP, :] for i in range(0, n, GROUP)]

    def column(x, at):
        return jnp.broadcast_to(x[:, at : at + 1], (GROUP, n))

    def row(x, at):
        return jnp.broadcast_to(x[at : at + 1, :], (GROUP, n))

    for b in range(n // GROUP):
        first = b * GROUP
        inside = (lane >= first) & (lane < first + GROUP)
        cols = [column(rows[b], first + j) for j in range(GROUP)]
        work = jnp.where(inside, jnp.where(lane - first == sub, 1.0, 0.0), rows[b])
        scale, scaled, cross = [], [], {}
        for k in range(GROUP):
            scale.append(lax.rsqrt(row(cols[k], k)))
            scaled.append(row(work, k) * scale[k])
            if k < GROUP - 1:
                factor = jnp.where(sub > k, cols[k] * scale[k], 0.0)
                for j in range(k + 1, GROUP):
                    cross[k, j] = row(cols[j], k) * scale[k]
                    cols[j] = cols[j] - factor * cross[k, j]
                work = work - factor * scaled[k]
        done = scaled[0]
        for k in range(1, GROUP):
            done = jnp.where(sub == k, scaled[k], done)
        out_ref[first : first + GROUP, :] = jnp.where(lane <= sub + first, done, 0.0)
        for i in range(b + 1, n // GROUP):
            cols = [column(rows[i], first + j) for j in range(GROUP)]
            rest = jnp.where(inside, 0.0, rows[i])
            for k in range(GROUP):
                factor = cols[k] * scale[k]
                for j in range(k + 1, GROUP):
                    cols[j] = cols[j] - factor * cross[k, j]
                rest = rest - factor * scaled[k]
            rows[i] = rest


def inverse_factor(diag_block):
    n = diag_block.shape[0]
    return pl.pallas_call(
        inverse_factor_kernel,
        out_shape=jax.ShapeDtypeStruct((n, n), jnp.float32),
        in_specs=[pl.BlockSpec(memory_space=pltpu.VMEM)],
        out_specs=pl.BlockSpec(memory_space=pltpu.VMEM),
        cost_estimate=pl.CostEstimate(flops=2_000_000_000, bytes_accessed=8 * n * n, transcendentals=n),
        compiler_params=pltpu.CompilerParams(vmem_limit_bytes=2 << 20),
        name="inverse_factor",
    )(diag_block)


class Plan:
    def __init__(self, prows, pcols, width, height, here):
        self.prows, self.pcols, self.height = prows, pcols, height
        self.step = min(width, height)
        spread = pcols // prows

        def strips(column):
            found = []
            for position in range(here):
                block = column // prows + position * spread
                for offset in range(0, width, self.step):
                    at = block * width + offset
                    found.append((at // height, at % height))
            return found

        self.total = here * width
        parity = [shard % 2 for shard, _ in strips(0)]
        assert parity == [s % 2 for s in range(len(parity))]
        self.strips_each = len(parity) // 2
        self.flips = []
        for row in range(prows):
            first = []
            for column in range(row, pcols, prows):
                for shard, _ in strips(column):
                    k = 2 * ((shard // 2) ^ (column // 2))
                    if k and k not in first:
                        first.append(k)
            first.sort(reverse=row < prows // 2 and False)
            first.sort(key=lambda k: (k != 4, -k))
            rest = [k for k in range(pcols - 2, 0, -2) if k not in first]
            self.flips.append([0] + first + rest)
        self.slots = pcols // 2
        self.starts = []
        last = 0
        for row in range(prows):
            for me in range(pcols):
                mine = [0] * self.strips_each
                for column in (me, me ^ 1):
                    if column % prows == row:
                        own = [s for s in strips(column) if s[0] % 2 == me % 2]
                        slot = [self.flips[row].index(2 * ((s // 2) ^ (me // 2))) for s, _ in own]
                        last = max(last, *slot)
                        mine = [j * height + at for j, (_, at) in zip(slot, own)]
                self.starts.append(mine)
        self.early = last + 1

    def pairs(self, slot):
        return [
            (row * self.pcols + i, row * self.pcols + (i ^ self.flips[row][slot]))
            for row in range(self.prows)
            for i in range(self.pcols)
        ]

    def pass_on(self, k):
        return [
            (row * self.pcols + i, (row ^ k) * self.pcols + i)
            for row in range(self.prows)
            for i in range(self.pcols)
            if row in (i % self.prows, (i ^ 1) % self.prows)
        ]


def pick(values, index):
    chosen = jnp.int32(values[0])
    for i, value in enumerate(values[1:], 1):
        chosen = jnp.where(index == i, jnp.int32(value), chosen)
    return chosen


def solve(rows, inverse):
    return lax.dot_general(rows, inverse, NT, precision=EXACT, preferred_element_type=jnp.float32)


def solve_kernel(plan, count, own, inverse_ref, *refs):
    piece_refs, refs = refs[:count], refs[count:]
    inverse = inverse_ref[...]
    for j, ref in enumerate(piece_refs):
        solved = solve(ref[...], inverse)
        if own and j == 0:
            refs[2][...] = solved
        refs[0][j * plan.height : (j + 1) * plan.height, :] = solved.astype(jnp.bfloat16)
    if own:
        device = lax.axis_index("prow") * plan.pcols + lax.axis_index("pcol")
        for s in range(plan.strips_each):
            start = pl.multiple_of(pick([v[s] for v in plan.starts], device), plan.step)
            refs[1][s * plan.step : (s + 1) * plan.step, :] = refs[0][pl.ds(start, plan.step), :]


def solve_pieces(plan, inverse, pieces, own):
    width = inverse.shape[0]
    count = len(pieces)
    vmem = pl.BlockSpec(memory_space=pltpu.VMEM)
    outs = [jax.ShapeDtypeStruct((count * plan.height, width), jnp.bfloat16)]
    if own:
        outs.append(jax.ShapeDtypeStruct((plan.strips_each * plan.step, width), jnp.bfloat16))
        outs.append(jax.ShapeDtypeStruct((plan.height, width), jnp.float32))
    return pl.pallas_call(
        functools.partial(solve_kernel, plan, count, own),
        out_shape=tuple(outs),
        in_specs=[vmem] * (count + 1),
        out_specs=tuple([vmem] * len(outs)),
        cost_estimate=pl.CostEstimate(
            flops=12 * count * plan.height * width * width, bytes_accessed=6 * count * plan.height * width, transcendentals=0
        ),
        compiler_params=pltpu.CompilerParams(vmem_limit_bytes=4 << 20),
        name="solve_own" if own else "solve_rest",
    )(inverse, *pieces)


def update_kernel(plan, groups, x_refs_n, *refs):
    x_refs, refs = refs[:x_refs_n], refs[x_refs_n:]
    mine_ref, other_ref, slab_ref, next_ref, column, out_vmem, sems = refs
    row, me = lax.axis_index("prow"), lax.axis_index("pcol")
    parity = lax.rem(me, 2)
    step = plan.step
    for s in range(plan.strips_each):
        for ref, side in ((mine_ref, parity), (other_ref, 1 - parity)):
            at = pl.multiple_of((2 * s + side) * step, step)
            column[pl.ds(at, step), :] = ref[s * step : (s + 1) * step, :]
    whole = column[...]
    flips = [pick([f[j] for f in plan.flips], row) for j in range(plan.slots)]
    copies = []
    for ref, (slots, side) in zip(x_refs, groups):
        for n, j in enumerate(slots):
            at = pl.ds(pl.multiple_of((me ^ side ^ flips[j]) * plan.height, plan.height), plan.height)
            product = lax.dot_general(
                ref[n * plan.height : (n + 1) * plan.height, :], whole, NT, preferred_element_type=jnp.float32
            )
            out_vmem[at, :] = slab_ref[at, :] - product
            copy = pltpu.make_async_copy(out_vmem.at[at, :], next_ref.at[at, :], sems.at[len(copies)])
            copy.start()
            copies.append(copy)
    for copy in copies:
        copy.wait()


def update(plan, groups, solved, mine, other, slab):
    vmem = pl.BlockSpec(memory_space=pltpu.VMEM)
    return pl.pallas_call(
        functools.partial(update_kernel, plan, groups, len(solved)),
        out_shape=jax.ShapeDtypeStruct(slab.shape, jnp.float32),
        in_specs=[vmem] * (len(solved) + 3),
        out_specs=pl.BlockSpec(memory_space=pl.ANY),
        scratch_shapes=[
            pltpu.VMEM((plan.total, mine.shape[1]), jnp.bfloat16),
            pltpu.VMEM(slab.shape, jnp.float32),
            pltpu.SemaphoreType.DMA((plan.pcols,)),
        ],
        cost_estimate=pl.CostEstimate(flops=300_000_000, bytes_accessed=8 * slab.size, transcendentals=0),
        compiler_params=pltpu.CompilerParams(vmem_limit_bytes=8 << 20),
        name="update",
    )(*solved, mine, other, slab)


def per_device(diag_block, panel, slab):
    prows = lax.axis_size("prow")
    pcols = lax.axis_size("pcol")
    width = diag_block.shape[0]
    plan = Plan(prows, pcols, width, panel.shape[0], slab.shape[1] // width)
    row, me = lax.axis_index("prow"), lax.axis_index("pcol")
    both = ("prow", "pcol")
    partner = [(i, i ^ 1) for i in range(pcols)]
    pieces = [panel]
    for j in range(1, plan.slots):
        pieces.append(lax.ppermute(panel, both, plan.pairs(j)))
    inverse = inverse_factor(diag_block)
    early, passed, factored = solve_pieces(plan, inverse, pieces[: plan.early], True)
    received = [passed]
    for k in range(1, prows):
        received.append(lax.ppermute(passed, both, plan.pass_on(k)))
    solved = [early]
    groups = [(tuple(range(plan.early)), 0)]
    if plan.early < plan.slots:
        (late,) = solve_pieces(plan, inverse, pieces[plan.early :], False)
        solved.append(late)
        groups.append((tuple(range(plan.early, plan.slots)), 0))
    for x, (slots, _) in zip(list(solved), list(groups)):
        solved.append(lax.ppermute(x, "pcol", partner))
        groups.append((slots, 1))

    def part(column):
        found = received[0]
        source = row ^ lax.rem(column, prows)
        for k in range(1, prows):
            found = jnp.where(source == k, received[k], found)
        return found

    mine = part(me)
    other = lax.ppermute(part(me ^ 1), "pcol", partner)
    slab_next = update(plan, groups, solved, mine, other, slab)
    return slab_next, factored


def solution(mesh):
    placed = (P(), P(("prow", "pcol"), None), P("prow", "pcol"))
    return jax.shard_map(
        per_device,
        mesh=mesh,
        in_specs=placed,
        out_specs=(P("prow", "pcol"), P(("prow", "pcol"), None)),
        check_vma=False,
    )
```

profile of v0, /device:TPU:0, one launch (start us, length us, event | category | flops | bytes accessed | tf_op | source)
XLA Modules:
  0.0 28.5 jit_solution(4315632377182019695)
XLA Ops:
  0.6 0.0 copy-start.1
  0.6 5.1 %collective-permute-start.1 = (f32[256,128]{1,0:T(8,128)}, f32[256,128]{1,0:T(8,128)S(1)}, u32[]{:S(2)}, u32[]{:S(2)}) collective-permute-start(f32[256,128]{1,0:T(8,128)} %refs_0_.1), channel_id=1, source_target_pairs={{0,6},{1,7},{2,4},{3,5},{4,2},{5,3},{6,0},{7,1},{8,14},{9,15},{10,... | collective-permute-start | bytes 393224 | tf_op jit(solution)/shard_map/ppermute | solution.py:235
  5.8 0.0 collective-permute-start
  5.8 0.6 %collective-permute-start.2 = (f32[256,128]{1,0:T(8,128)}, f32[256,128]{1,0:T(8,128)S(1)}, u32[]{:S(2)}, u32[]{:S(2)}) collective-permute-start(f32[256,128]{1,0:T(8,128)} %refs_0_.1), channel_id=1, source_target_pairs={{0,2},{1,3},{2,0},{3,1},{4,6},{5,7},{6,4},{7,5},{8,10},{9,11},{10,... | collective-permute-start | bytes 393224 | tf_op jit(solution)/shard_map/ppermute | solution.py:235
  6.4 0.0 copy-start.2
  6.4 0.8 %copy-done.2 = f32[128,128]{1,0:T(8,128)S(1)} copy-done((f32[128,128]{1,0:T(8,128)S(1)}, f32[128,128]{1,0:T(8,128)}, u32[]{:S(2)}) %copy-start.2) | copy-done | bytes 65560
  7.3 0.0 copy-start
  7.3 3.8 %inverse_factor.1.inverse_ref = f32[128,128]{1,0:T(8,128)S(1)} custom-call(f32[128,128]{1,0:T(8,128)S(1)} %copy-done.2), custom_call_target="tpu_custom_call" | custom-call | flops 2000000000 | bytes 131072 | tf_op jit(solution)/shard_map/inverse_factor/pallas_call | solution.py:60
  11.1 0.0 collective-permute-done.1.refs_2_
  11.1 5.9 %collective-permute-done.refs_1_ = f32[256,128]{1,0:T(8,128)S(1)} collective-permute-done((f32[256,128]{1,0:T(8,128)}, f32[256,128]{1,0:T(8,128)S(1)}, u32[]{:S(2)}, u32[]{:S(2)}) %collective-permute-start) | collective-permute-done | bytes 131104 | tf_op jit(solution)/shard_map/ppermute | solution.py:235
  17.1 0.0 copy-done.1
  17.1 0.9 %solve_own.1 = (bf16[768,128]{1,0:T(8,128)(2,1)S(1)}, bf16[128,128]{1,0:T(8,128)(2,1)S(1)}, f32[256,128]{1,0:T(8,128)}) custom-call(f32[128,128]{1,0:T(8,128)S(1)} %inverse_factor.1.inverse_ref, f32[256,128]{1,0:T(8,128)S(1)} %copy-done.1, f32[256,128]{1,0:T(8,128)S(1)} %collective-permute-done.refs_1_, f32[256,128]{1,0:T(8,128)S(1)} %collective-permute-done.1.refs_2_), custom_call_target="tpu_custom_call" | custom-call | flops 150994944 | bytes 589824 | tf_op jit(solution)/shard_map/solve_own/pallas_call | solution.py:167
  18.0 3.4 %collective-permute-start.7 = (bf16[128,128]{1,0:T(8,128)(2,1)S(1)}, bf16[128,128]{1,0:T(8,128)(2,1)S(1)}, u32[]{:S(2)}, u32[]{:S(2)}) collective-permute-start(bf16[128,128]{1,0:T(8,128)(2,1)S(1)} %get-tuple-element.6), channel_id=1, source_target_pairs={{0,8},{1,9},{4,12},{5,13},{8,0},{9,1},{12,4},{13,5},{18,26},{19,27... | collective-permute-start | bytes 98312 | tf_op jit(solution)/shard_map/ppermute | solution.py:240
  21.4 1.3 %collective-permute-start.6 = (bf16[128,128]{1,0:T(8,128)(2,1)S(1)}, bf16[128,128]{1,0:T(8,128)(2,1)S(1)}, u32[]{:S(2)}, u32[]{:S(2)}) collective-permute-start(bf16[128,128]{1,0:T(8,128)(2,1)S(1)} %get-tuple-element.6), channel_id=1, source_target_pairs={{0,16},{1,17},{4,20},{5,21},{8,24},{9,25},{12,28},{13,29},{18,2},{... | collective-permute-start | bytes 98312 | tf_op jit(solution)/shard_map/ppermute | solution.py:240
  22.7 1.3 %collective-permute-start.5 = (bf16[128,128]{1,0:T(8,128)(2,1)S(1)}, bf16[128,128]{1,0:T(8,128)(2,1)S(1)}, u32[]{:S(2)}, u32[]{:S(2)}) collective-permute-start(bf16[128,128]{1,0:T(8,128)(2,1)S(1)} %get-tuple-element.6), channel_id=1, source_target_pairs={{0,24},{1,25},{4,28},{5,29},{8,16},{9,17},{12,20},{13,21},{18,10},... | collective-permute-start | bytes 98312 | tf_op jit(solution)/shard_map/ppermute | solution.py:240
  24.0 0.0 collective-permute-done.2.refs_0_
  24.0 0.3 solve_rest.1.refs_1_
  24.3 0.1 collective-permute-start.4
  24.4 0.5 %collective-permute-start.3 = (bf16[768,128]{1,0:T(8,128)(2,1)S(1)}, bf16[768,128]{1,0:T(8,128)(2,1)S(1)}, u32[]{:S(2)}, u32[]{:S(2)}) collective-permute-start(bf16[768,128]{1,0:T(8,128)(2,1)S(1)} %get-tuple-element.5.refs_0_), channel_id=1, source_target_pairs={{0,1},{1,0},{2,3},{3,2},{4,5},{5,4},{6,7},{7,6},{8,9},{9,8},{10,11... | collective-permute-start | bytes 589832 | tf_op jit(solution)/shard_map/ppermute | solution.py:248
  24.9 0.0 collective-permute-done.7
  24.9 0.0 collective-permute-done.6
  24.9 0.7 %collective-permute-done.5 = bf16[128,128]{1,0:T(8,128)(2,1)S(1)} collective-permute-done((bf16[128,128]{1,0:T(8,128)(2,1)S(1)}, bf16[128,128]{1,0:T(8,128)(2,1)S(1)}, u32[]{:S(2)}, u32[]{:S(2)}) %collective-permute-start.5) | collective-permute-done | bytes 32800 | tf_op jit(solution)/shard_map/ppermute | solution.py:240
  25.6 0.1 collective-permute-start.8
  25.7 0.0 collective-permute-done.4.refs_3_
  25.7 1.2 %collective-permute-done.8.refs_5_ = bf16[128,128]{1,0:T(8,128)(2,1)S(1)} collective-permute-done((bf16[128,128]{1,0:T(8,128)(2,1)S(1)}, bf16[128,128]{1,0:T(8,128)(2,1)S(1)}, u32[]{:S(2)}, u32[]{:S(2)}) %collective-permute-start.8) | collective-permute-done | bytes 32800 | tf_op jit(solution)/shard_map/ppermute | solution.py:259
  26.9 0.0 collective-permute-done.3.refs_2_
  26.9 0.0 copy-done
  26.9 1.6 %update.1 = f32[2048,256]{1,0:T(8,128)} custom-call(bf16[768,128]{1,0:T(8,128)(2,1)S(1)} %get-tuple-element.5.refs_0_, bf16[256,128]{1,0:T(8,128)(2,1)S(1)} %solve_rest.1.refs_1_, bf16[768,128]{1,0:T(8,128)(2,1)S(1)} %collective-permute-done.3.refs_2_, bf16[256,128]{1,0:T(8,128)(2,1)S(1)} %collective-permute-done.4.refs_3_, ...), custom_call_target="tpu_custom_call" | custom-call | flops 300000000 | bytes 4194304 | tf_op jit(solution)/shard_map/update/pallas_call | solution.py:209
  (1 shorter events, 0.0 us)
Async XLA Ops:
  0.6 16.4 %copy-start.1 = (f32[256,128]{1,0:T(8,128)S(1)}, f32[256,128]{1,0:T(8,128)}, u32[]{:S(2)}) copy-start(f32[256,128]{1,0:T(8,128)} %refs_0_.1) | copy-start | bytes 393220
  0.6 10.5 %collective-permute-start.1 = (f32[256,128]{1,0:T(8,128)}, f32[256,128]{1,0:T(8,128)S(1)}, u32[]{:S(2)}, u32[]{:S(2)}) collective-permute-start(f32[256,128]{1,0:T(8,128)} %refs_0_.1), channel_id=1, source_target_pairs={{0,6},{1,7},{2,4},{3,5},{4,2},{5,3},{6,0},{7,1},{8,14},{9,15},{10,... | collective-permute-start | bytes 393224 | tf_op jit(solution)/shard_map/ppermute | solution.py:235
  5.8 11.3 %collective-permute-start = (f32[256,128]{1,0:T(8,128)}, f32[256,128]{1,0:T(8,128)S(1)}, u32[]{:S(2)}, u32[]{:S(2)}) collective-permute-start(f32[256,128]{1,0:T(8,128)} %refs_0_.1), channel_id=1, source_target_pairs={{0,4},{1,5},{2,6},{3,7},{4,0},{5,1},{6,2},{7,3},{8,12},{9,13},{10,... | collective-permute-start | bytes 393224 | tf_op jit(solution)/shard_map/ppermute | solution.py:235
  5.8 18.2 %collective-permute-start.2 = (f32[256,128]{1,0:T(8,128)}, f32[256,128]{1,0:T(8,128)S(1)}, u32[]{:S(2)}, u32[]{:S(2)}) collective-permute-start(f32[256,128]{1,0:T(8,128)} %refs_0_.1), channel_id=1, source_target_pairs={{0,2},{1,3},{2,0},{3,1},{4,6},{5,7},{6,4},{7,5},{8,10},{9,11},{10,... | collective-permute-start | bytes 393224 | tf_op jit(solution)/shard_map/ppermute | solution.py:235
  6.4 0.8 %copy-start.2 = (f32[128,128]{1,0:T(8,128)S(1)}, f32[128,128]{1,0:T(8,128)}, u32[]{:S(2)}) copy-start(f32[128,128]{1,0:T(8,128)} %diag_ref.1) | copy-start | bytes 196612
  7.3 19.6 %copy-start = (f32[2048,256]{1,0:T(8,128)S(1)}, f32[2048,256]{1,0:T(8,128)}, u32[]{:S(2)}) copy-start(f32[2048,256]{1,0:T(8,128)} %refs_6_.1) | copy-start | bytes 6291460
  18.0 6.9 %collective-permute-start.7 = (bf16[128,128]{1,0:T(8,128)(2,1)S(1)}, bf16[128,128]{1,0:T(8,128)(2,1)S(1)}, u32[]{:S(2)}, u32[]{:S(2)}) collective-permute-start(bf16[128,128]{1,0:T(8,128)(2,1)S(1)} %get-tuple-element.6), channel_id=1, source_target_pairs={{0,8},{1,9},{4,12},{5,13},{8,0},{9,1},{12,4},{13,5},{18,26},{19,27... | collective-permute-start | bytes 98312 | tf_op jit(solution)/shard_map/ppermute | solution.py:240
  21.4 3.5 %collective-permute-start.6 = (bf16[128,128]{1,0:T(8,128)(2,1)S(1)}, bf16[128,128]{1,0:T(8,128)(2,1)S(1)}, u32[]{:S(2)}, u32[]{:S(2)}) collective-permute-start(bf16[128,128]{1,0:T(8,128)(2,1)S(1)} %get-tuple-element.6), channel_id=1, source_target_pairs={{0,16},{1,17},{4,20},{5,21},{8,24},{9,25},{12,28},{13,29},{18,2},{... | collective-permute-start | bytes 98312 | tf_op jit(solution)/shard_map/ppermute | solution.py:240
  22.7 2.9 %collective-permute-start.5 = (bf16[128,128]{1,0:T(8,128)(2,1)S(1)}, bf16[128,128]{1,0:T(8,128)(2,1)S(1)}, u32[]{:S(2)}, u32[]{:S(2)}) collective-permute-start(bf16[128,128]{1,0:T(8,128)(2,1)S(1)} %get-tuple-element.6), channel_id=1, source_target_pairs={{0,24},{1,25},{4,28},{5,29},{8,16},{9,17},{12,20},{13,21},{18,10},... | collective-permute-start | bytes 98312 | tf_op jit(solution)/shard_map/ppermute | solution.py:240
  24.3 1.4 %collective-permute-start.4 = (bf16[256,128]{1,0:T(8,128)(2,1)S(1)}, bf16[256,128]{1,0:T(8,128)(2,1)S(1)}, u32[]{:S(2)}, u32[]{:S(2)}) collective-permute-start(bf16[256,128]{1,0:T(8,128)(2,1)S(1)} %solve_rest.1.refs_1_), channel_id=1, source_target_pairs={{0,1},{1,0},{2,3},{3,2},{4,5},{5,4},{6,7},{7,6},{8,9},{9,8},{10,11... | collective-permute-start | bytes 196616 | tf_op jit(solution)/shard_map/ppermute | solution.py:248
  24.4 2.5 %collective-permute-start.3 = (bf16[768,128]{1,0:T(8,128)(2,1)S(1)}, bf16[768,128]{1,0:T(8,128)(2,1)S(1)}, u32[]{:S(2)}, u32[]{:S(2)}) collective-permute-start(bf16[768,128]{1,0:T(8,128)(2,1)S(1)} %get-tuple-element.5.refs_0_), channel_id=1, source_target_pairs={{0,1},{1,0},{2,3},{3,2},{4,5},{5,4},{6,7},{7,6},{8,9},{9,8},{10,11... | collective-permute-start | bytes 589832 | tf_op jit(solution)/shard_map/ppermute | solution.py:248
  25.6 1.3 %collective-permute-start.8 = (bf16[128,128]{1,0:T(8,128)(2,1)S(1)}, bf16[128,128]{1,0:T(8,128)(2,1)S(1)}, u32[]{:S(2)}, u32[]{:S(2)}) collective-permute-start(bf16[128,128]{1,0:T(8,128)(2,1)S(1)} %get-tuple-element.8), channel_id=1, source_target_pairs={{0,1},{1,0},{2,3},{3,2},{4,5},{5,4},{6,7},{7,6},{8,9},{9,8},{10,11... | collective-permute-start | bytes 98312 | tf_op jit(solution)/shard_map/ppermute | solution.py:259
where the time goes:
time: 28.7 us; the launch traced here: 28.5 us
  starting transfers between devices  12.4 us (43%)
  waiting for transfers between devices  7.82 us (27%)
  Pallas kernels  6.67 us (23%)
  local copies, waits for them, and re-layouts  0.85 us (3%)
  between operations  0.75 us (3%)
    ppermute x3, starting transfers between devices, per_device(): received.append(lax.ppermute(passed, both, plan.pass_on(k)))  5.97 us
    ppermute x3, waiting for transfers between devices, per_device(): pieces.append(lax.ppermute(panel, both, plan.pairs(j)))  5.95 us
    ppermute x3, starting transfers between devices, per_device(): pieces.append(lax.ppermute(panel, both, plan.pairs(j)))  5.78 us
    pallas_call x1, Pallas kernels, inverse_factor(): pl.pallas_call(inverse_factor_kernel, out_shape=jax.ShapeDtypeStruct((n,...  3.83 us
    pallas_call x1, Pallas kernels, update(): pl.pallas_call(functools.partial(update_kernel, plan, groups, len(solved)...  1.62 us
    pallas_call x2, Pallas kernels, solve_pieces(): pl.pallas_call(functools.partial(solve_kernel, plan, count, own), out_sha...  1.22 us
    ppermute x1, waiting for transfers between devices, per_device(): other = lax.ppermute(part(me ^ 1), 'pcol', partner)  1.18 us
    unnamed x6, local copies, waits for them, and re-layouts  0.85 us
  transfers between devices with their start and end apart: 9, of which 3 were waited for; matrix products, arithmetic and copies ran while one was open for 0% of the time, Pallas kernels for 18%

commit v1 on v0

v1 whole, which is shorter than its diff:
```python
import functools

import jax
import jax.numpy as jnp
from jax import lax
from jax.experimental import pallas as pl
from jax.experimental.pallas import tpu as pltpu
from jax.sharding import PartitionSpec as P


GROUP = 8
EXACT = lax.Precision.HIGHEST
NT = (((1,), (1,)), ((), ()))


def invert_factor(diag_ref, out_ref):
    n = diag_ref.shape[0]
    lane = lax.broadcasted_iota(jnp.int32, (GROUP, n), 1)
    sub = lax.broadcasted_iota(jnp.int32, (GROUP, n), 0)
    rows = [diag_ref[i : i + GROUP, :] for i in range(0, n, GROUP)]

    def column(x, at):
        return jnp.broadcast_to(x[:, at : at + 1], (GROUP, n))

    def row(x, at):
        return jnp.broadcast_to(x[at : at + 1, :], (GROUP, n))

    for b in range(n // GROUP):
        first = b * GROUP
        inside = (lane >= first) & (lane < first + GROUP)
        cols = [column(rows[b], first + j) for j in range(GROUP)]
        work = jnp.where(inside, jnp.where(lane - first == sub, 1.0, 0.0), rows[b])
        scale, scaled, cross = [], [], {}
        for k in range(GROUP):
            scale.append(lax.rsqrt(row(cols[k], k)))
            scaled.append(row(work, k) * scale[k])
            if k < GROUP - 1:
                factor = jnp.where(sub > k, cols[k] * scale[k], 0.0)
                for j in range(k + 1, GROUP):
                    cross[k, j] = row(cols[j], k) * scale[k]
                    cols[j] = cols[j] - factor * cross[k, j]
                work = work - factor * scaled[k]
        done = scaled[0]
        for k in range(1, GROUP):
            done = jnp.where(sub == k, scaled[k], done)
        out_ref[first : first + GROUP, :] = jnp.where(lane <= sub + first, done, 0.0)
        for i in range(b + 1, n // GROUP):
            cols = [column(rows[i], first + j) for j in range(GROUP)]
            rest = jnp.where(inside, 0.0, rows[i])
            for k in range(GROUP):
                factor = cols[k] * scale[k]
                for j in range(k + 1, GROUP):
                    cols[j] = cols[j] - factor * cross[k, j]
                rest = rest - factor * scaled[k]
            rows[i] = rest


def solve_kernel(diag_ref, panel_ref, factored_ref, low_ref, inverse):
    invert_factor(diag_ref, inverse)
    solved = lax.dot_general(
        panel_ref[...], inverse[...], NT, precision=EXACT, preferred_element_type=jnp.float32
    )
    factored_ref[...] = solved
    low_ref[...] = solved.astype(jnp.bfloat16)


def solve_panel(diag_block, panel):
    vmem = pl.BlockSpec(memory_space=pltpu.VMEM)
    return pl.pallas_call(
        solve_kernel,
        out_shape=(
            jax.ShapeDtypeStruct(panel.shape, jnp.float32),
            jax.ShapeDtypeStruct(panel.shape, jnp.bfloat16),
        ),
        in_specs=[vmem, vmem],
        out_specs=(vmem, vmem),
        scratch_shapes=[pltpu.VMEM(diag_block.shape, jnp.float32)],
        cost_estimate=pl.CostEstimate(flops=2_000_000_000, bytes_accessed=8 * panel.size, transcendentals=0),
        compiler_params=pltpu.CompilerParams(vmem_limit_bytes=2 << 20),
        name="solve_panel",
    )(diag_block, panel)


class Plan:
    def __init__(self, prows, pcols, width, height, here):
        self.prows, self.pcols, self.height = prows, pcols, height
        self.step = min(width, height)
        spread = pcols // prows

        def strips(column):
            found = []
            for position in range(here):
                block = column // prows + position * spread
                for offset in range(0, width, self.step):
                    at = block * width + offset
                    found.append((at // height, at % height))
            return found

        self.total = here * width
        parity = [shard % 2 for shard, _ in strips(0)]
        assert parity == [s % 2 for s in range(len(parity))]
        self.strips_each = len(parity) // 2
        self.slots = pcols // 2
        self.flips = []
        for row in range(prows):
            first = []
            for column in range(row, pcols, prows):
                for shard, _ in strips(column):
                    k = 2 * ((shard // 2) ^ (column // 2))
                    if k and k not in first:
                        first.append(k)
            first.sort(reverse=True)
            rest = [k for k in range(2, pcols, 2) if k not in first]
            self.flips.append([0] + first + rest)
        self.places = [[None] * (prows * pcols) for _ in range(self.strips_each)]
        for row in range(prows):
            for me in range(pcols):
                for column in (me, me ^ 1):
                    if column % prows == row:
                        own = [s for s in strips(column) if s[0] % 2 == me % 2]
                        for n, (shard, at) in enumerate(own):
                            slot = self.flips[row].index(2 * ((shard // 2) ^ (me // 2)))
                            self.places[n][row * pcols + me] = (slot, at)

    def pairs(self, slot):
        return [
            (row * self.pcols + i, row * self.pcols + (i ^ self.flips[row][slot]))
            for row in range(self.prows)
            for i in range(self.pcols)
        ]


def pick(values, index):
    chosen = jnp.int32(values[0])
    for i, value in enumerate(values[1:], 1):
        chosen = jnp.where(index == i, jnp.int32(value), chosen)
    return chosen


def update_kernel(plan, count, *refs):
    x_refs, refs = refs[:count], refs[count:]
    mine_ref, other_ref, slab_ref, next_ref, column, out_vmem, sems = refs
    row, me = lax.axis_index("prow"), lax.axis_index("pcol")
    parity = lax.rem(me, 2)
    step = plan.step
    for s in range(plan.strips_each):
        for ref, side in ((mine_ref, parity), (other_ref, 1 - parity)):
            at = pl.multiple_of((2 * s + side) * step, step)
            column[pl.ds(at, step), :] = ref[s * step : (s + 1) * step, :]
    whole = column[...]
    flips = [pick([f[j] for f in plan.flips], row) for j in range(plan.slots)]
    copies = []
    for n, ref in enumerate(x_refs):
        from_column = me ^ flips[n % plan.slots] ^ (n // plan.slots)
        at = pl.ds(pl.multiple_of(from_column * plan.height, plan.height), plan.height)
        product = lax.dot_general(ref[...], whole, NT, preferred_element_type=jnp.float32)
        out_vmem[at, :] = slab_ref[at, :] - product
        copy = pltpu.make_async_copy(out_vmem.at[at, :], next_ref.at[at, :], sems.at[n])
        copy.start()
        copies.append(copy)
    for copy in copies:
        copy.wait()


def update(plan, solved, mine, other, slab):
    vmem = pl.BlockSpec(memory_space=pltpu.VMEM)
    return pl.pallas_call(
        functools.partial(update_kernel, plan, len(solved)),
        out_shape=jax.ShapeDtypeStruct(slab.shape, jnp.float32),
        in_specs=[vmem] * (len(solved) + 3),
        out_specs=pl.BlockSpec(memory_space=pl.ANY),
        scratch_shapes=[
            pltpu.VMEM((plan.total, mine.shape[1]), jnp.bfloat16),
            pltpu.VMEM(slab.shape, jnp.float32),
            pltpu.SemaphoreType.DMA((plan.pcols,)),
        ],
        cost_estimate=pl.CostEstimate(flops=300_000_000, bytes_accessed=8 * slab.size, transcendentals=0),
        compiler_params=pltpu.CompilerParams(vmem_limit_bytes=8 << 20),
        name="update",
    )(*solved, mine, other, slab)


def choose(options, index):
    chosen = options[0][0]
    for value, indices in options[1:]:
        hit = index == indices[0]
        for i in indices[1:]:
            hit = hit | (index == i)
        chosen = jnp.where(hit, value, chosen)
    return chosen


def per_device(diag_block, panel, slab):
    prows = lax.axis_size("prow")
    pcols = lax.axis_size("pcol")
    width = diag_block.shape[0]
    plan = Plan(prows, pcols, width, panel.shape[0], slab.shape[1] // width)
    row, me = lax.axis_index("prow"), lax.axis_index("pcol")
    device = row * pcols + me
    both = ("prow", "pcol")
    partner = [(i, i ^ 1) for i in range(pcols)]
    factored, low = solve_panel(diag_block, panel)
    solved = [low]
    for j in range(1, plan.slots):
        solved.append(lax.ppermute(low, both, plan.pairs(j)))

    strips = []
    for places in plan.places:
        options = {}
        for at, place in enumerate(places):
            if place is not None:
                options.setdefault(place, []).append(at)
        strips.append(choose([(solved[j][at : at + plan.step], where) for (j, at), where in options.items()], device))
    passed = jnp.concatenate(strips, 0) if len(strips) > 1 else strips[0]
    received = [(passed, [0])]
    for k in range(1, prows):
        received.append((lax.ppermute(passed, "prow", [(i, i ^ k) for i in range(prows)]), [k]))
    for j in range(plan.slots):
        solved.append(lax.ppermute(solved[j], "pcol", partner))
    mine = choose(received, row ^ lax.rem(me, prows))
    other = lax.ppermute(choose(received, row ^ lax.rem(me ^ 1, prows)), "pcol", partner)
    slab_next = update(plan, solved, mine, other, slab)
    return slab_next, factored


def solution(mesh):
    placed = (P(), P(("prow", "pcol"), None), P("prow", "pcol"))
    return jax.shard_map(
        per_device,
        mesh=mesh,
        in_specs=placed,
        out_specs=(P("prow", "pcol"), P(("prow", "pcol"), None)),
        check_vma=False,
    )
```

time: 28.7 us -> 28.2 us (0.983)
  starting transfers between devices: 12.4 us -> 9.85 us
  waiting for transfers between devices: 7.82 us -> 9.19 us
  local copies, waits for them, and re-layouts: 0.85 us -> 1.74 us
    ppermute x9 -> x11, starting transfers between devices: 12.4 us -> 9.85 us  [the longest x3 5.64 us: per_device(): solved.append(lax.ppermute(low, both, plan.pairs(j)))]
    ppermute x9 -> x11, waiting for transfers between devices: 7.82 us -> 9.19 us  [the longest x3 4.67 us: per_device(): solved.append(lax.ppermute(low, both, plan.pairs(j)))]
    unnamed x6, local copies, waits for them, and re-layouts: 0.85 us -> 1.74 us
    pallas_call x4 -> x2, Pallas kernels: 6.67 us -> 6.5 us  [the longest x1 4.88 us: solve_panel(): pl.pallas_call(solve_kernel, out_shape=(jax.ShapeDtypeStruct(panel.shape,...]
  transfers between devices with their start and end apart: 9 -> 11, of which waited for: 3 -> 4; matrix products, arithmetic and copies ran while one was open for 0% -> 0% of each run, Pallas kernels for 18% -> 0%
where the time goes in v1:
time: 28.2 us; the launch traced here: 28 us
  starting transfers between devices  9.85 us (35%)
  waiting for transfers between devices  9.19 us (33%)
  Pallas kernels  6.5 us (23%)
  local copies, waits for them, and re-layouts  1.74 us (6%)
  between operations  0.69 us (2%)
    ppermute x3, starting transfers between devices, per_device(): solved.append(lax.ppermute(low, both, plan.pairs(j)))  5.64 us
    pallas_call x1, Pallas kernels, solve_panel(): pl.pallas_call(solve_kernel, out_shape=(jax.ShapeDtypeStruct(panel.shape,...  4.88 us
    ppermute x3, waiting for transfers between devices, per_device(): solved.append(lax.ppermute(low, both, plan.pairs(j)))  4.67 us
    ppermute x3, starting transfers between devices, per_device(): lax.ppermute(passed, 'prow', [(i, i ^ k) for i in range(prows)])  3.55 us
    ppermute x3, waiting for transfers between devices, per_device(): lax.ppermute(passed, 'prow', [(i, i ^ k) for i in range(prows)])  3.35 us
    unnamed x6, local copies, waits for them, and re-layouts  1.74 us
    pallas_call x1, Pallas kernels, update(): pl.pallas_call(functools.partial(update_kernel, plan, len(solved)), out_s...  1.63 us
    ppermute x1, waiting for transfers between devices, per_device(): lax.ppermute(choose(received, row ^ lax.rem(me ^ 1, prows)), 'pcol', part...  1.16 us
  transfers between devices with their start and end apart: 11, of which 4 were waited for; matrix products, arithmetic and copies ran while one was open for 0% of the time, Pallas kernels for 0%

profile of v1, /device:TPU:0, one launch (start us, length us, event | category | flops | bytes accessed | tf_op | source)
XLA Modules:
  0.0 28.0 jit_solution(15959974896033075522)
XLA Ops:
  0.6 0.0 copy-start.1
  0.6 0.9 %copy-done.1 = f32[256,128]{1,0:T(8,128)S(1)} copy-done((f32[256,128]{1,0:T(8,128)S(1)}, f32[256,128]{1,0:T(8,128)}, u32[]{:S(2)}) %copy-start.1) | copy-done | bytes 131096
  1.5 0.0 copy-start.2
  1.5 0.8 %copy-done.2 = f32[128,128]{1,0:T(8,128)S(1)} copy-done((f32[128,128]{1,0:T(8,128)S(1)}, f32[128,128]{1,0:T(8,128)}, u32[]{:S(2)}) %copy-start.2) | copy-done | bytes 65560
  2.4 0.0 copy-start
  2.4 4.9 %solve_panel.1 = (f32[256,128]{1,0:T(8,128)}, bf16[256,128]{1,0:T(8,128)(2,1)S(1)}) custom-call(f32[128,128]{1,0:T(8,128)S(1)} %copy-done.2, f32[256,128]{1,0:T(8,128)S(1)} %copy-done.1), custom_call_target="tpu_custom_call" | custom-call | flops 2000000000 | bytes 262144 | tf_op jit(solution)/shard_map/solve_panel/pallas_call | solution.py:69
  7.3 3.1 %collective-permute-start.1 = (bf16[256,128]{1,0:T(8,128)(2,1)S(1)}, bf16[256,128]{1,0:T(8,128)(2,1)S(1)}, u32[]{:S(2)}, u32[]{:S(2)}) collective-permute-start(bf16[256,128]{1,0:T(8,128)(2,1)S(1)} %get-tuple-element.4.refs_0_), channel_id=1, source_target_pairs={{0,2},{1,3},{2,0},{3,1},{4,6},{5,7},{6,4},{7,5},{8,10},{9,11},{10,... | collective-permute-start | bytes 196616 | tf_op jit(solution)/shard_map/ppermute | solution.py:205
  10.3 2.6 %collective-permute-start = (bf16[256,128]{1,0:T(8,128)(2,1)S(1)}, bf16[256,128]{1,0:T(8,128)(2,1)S(1)}, u32[]{:S(2)}, u32[]{:S(2)}) collective-permute-start(bf16[256,128]{1,0:T(8,128)(2,1)S(1)} %get-tuple-element.4.refs_0_), channel_id=1, source_target_pairs={{0,4},{1,5},{2,6},{3,7},{4,0},{5,1},{6,2},{7,3},{8,12},{9,13},{10,... | collective-permute-start | bytes 196616 | tf_op jit(solution)/shard_map/ppermute | solution.py:205
  12.9 0.0 collective-permute-start.2
  12.9 0.0 collective-permute-done.1.refs_2_
  12.9 4.7 %collective-permute-done.refs_1_ = bf16[256,128]{1,0:T(8,128)(2,1)S(1)} collective-permute-done((bf16[256,128]{1,0:T(8,128)(2,1)S(1)}, bf16[256,128]{1,0:T(8,128)(2,1)S(1)}, u32[]{:S(2)}, u32[]{:S(2)}) %collective-permute-start) | collective-permute-done | bytes 65568 | tf_op jit(solution)/shard_map/ppermute | solution.py:205
  17.6 1.6 %collective-permute-start.9 = (bf16[128,128]{1,0:T(8,128)(2,1)S(1)}, bf16[128,128]{1,0:T(8,128)(2,1)S(1)}, u32[]{:S(2)}, u32[]{:S(2)}) collective-permute-start(bf16[128,128]{1,0:T(8,128)(2,1)S(1)} %fusion), channel_id=1, source_target_pairs={{0,8},{8,0},{16,24},{24,16},{1,9},{9,1},{17,25},{25,17},{2,10},{10... | collective-permute-start | bytes 98312 | tf_op jit(solution)/shard_map/ppermute | solution.py:217
  19.1 1.1 %collective-permute-start.8 = (bf16[128,128]{1,0:T(8,128)(2,1)S(1)}, bf16[128,128]{1,0:T(8,128)(2,1)S(1)}, u32[]{:S(2)}, u32[]{:S(2)}) collective-permute-start(bf16[128,128]{1,0:T(8,128)(2,1)S(1)} %fusion), channel_id=1, source_target_pairs={{0,16},{8,24},{16,0},{24,8},{1,17},{9,25},{17,1},{25,9},{2,18},{10... | collective-permute-start | bytes 98312 | tf_op jit(solution)/shard_map/ppermute | solution.py:217
  20.3 0.9 %collective-permute-start.7 = (bf16[128,128]{1,0:T(8,128)(2,1)S(1)}, bf16[128,128]{1,0:T(8,128)(2,1)S(1)}, u32[]{:S(2)}, u32[]{:S(2)}) collective-permute-start(bf16[128,128]{1,0:T(8,128)(2,1)S(1)} %fusion), channel_id=1, source_target_pairs={{0,24},{8,16},{16,8},{24,0},{1,25},{9,17},{17,9},{25,1},{2,26},{10... | collective-permute-start | bytes 98312 | tf_op jit(solution)/shard_map/ppermute | solution.py:217
  21.1 0.0 collective-permute-start.3
  21.1 0.0 collective-permute-done.2.refs_3_
  21.1 0.5 %collective-permute-start.5 = (bf16[256,128]{1,0:T(8,128)(2,1)S(1)}, bf16[256,128]{1,0:T(8,128)(2,1)S(1)}, u32[]{:S(2)}, u32[]{:S(2)}) collective-permute-start(bf16[256,128]{1,0:T(8,128)(2,1)S(1)} %collective-permute-done.1.refs_2_), channel_id=1, source_target_pairs={{0,1},{1,0},{2,3},{3,2},{4,5},{5,4},{6,7},{7,6},{8,9},{9,8},{10,11... | collective-permute-start | bytes 196616 | tf_op jit(solution)/shard_map/ppermute | solution.py:219
  21.7 0.0 collective-permute-done.9
  21.7 0.1 collective-permute-start.4
  21.7 1.3 %collective-permute-done.8 = bf16[128,128]{1,0:T(8,128)(2,1)S(1)} collective-permute-done((bf16[128,128]{1,0:T(8,128)(2,1)S(1)}, bf16[128,128]{1,0:T(8,128)(2,1)S(1)}, u32[]{:S(2)}, u32[]{:S(2)}) %collective-permute-start.8) | collective-permute-done | bytes 32800 | tf_op jit(solution)/shard_map/ppermute | solution.py:217
  23.1 0.0 collective-permute-start.6
  23.1 2.0 %collective-permute-done.7 = bf16[128,128]{1,0:T(8,128)(2,1)S(1)} collective-permute-done((bf16[128,128]{1,0:T(8,128)(2,1)S(1)}, bf16[128,128]{1,0:T(8,128)(2,1)S(1)}, u32[]{:S(2)}, u32[]{:S(2)}) %collective-permute-start.7) | collective-permute-done | bytes 32800 | tf_op jit(solution)/shard_map/ppermute | solution.py:217
  25.1 0.1 collective-permute-start.10
  25.2 0.0 collective-permute-done.3.refs_4_
  25.2 0.0 collective-permute-done.6.refs_7_
  25.2 0.0 collective-permute-done.5.refs_6_
  25.2 1.2 %collective-permute-done.10.refs_9_ = bf16[128,128]{1,0:T(8,128)(2,1)S(1)} collective-permute-done((bf16[128,128]{1,0:T(8,128)(2,1)S(1)}, bf16[128,128]{1,0:T(8,128)(2,1)S(1)}, u32[]{:S(2)}, u32[]{:S(2)}) %collective-permute-start.10) | collective-permute-done | bytes 32800 | tf_op jit(solution)/shard_map/ppermute | solution.py:221
  26.4 0.0 collective-permute-done.4.refs_5_
  26.4 0.0 copy-done
  26.4 1.6 %update.1 = f32[2048,256]{1,0:T(8,128)} custom-call(bf16[256,128]{1,0:T(8,128)(2,1)S(1)} %get-tuple-element.4.refs_0_, bf16[256,128]{1,0:T(8,128)(2,1)S(1)} %collective-permute-done.refs_1_, bf16[256,128]{1,0:T(8,128)(2,1)S(1)} %collective-permute-done.1.refs_2_, bf16[256,128]{1,0:T(8,128)(2,1)S(1)} %collective-permute-done.2.refs_3_, ...), custom_call_target="tpu_custom_call" | custom-call | flops 300000000 | bytes 4194304 | tf_op jit(solution)/shard_map/update/pallas_call | solution.py:167
  (2 shorter events, 0.0 us)
Async XLA Ops:
  0.6 0.9 %copy-start.1 = (f32[256,128]{1,0:T(8,128)S(1)}, f32[256,128]{1,0:T(8,128)}, u32[]{:S(2)}) copy-start(f32[256,128]{1,0:T(8,128)} %panel_ref.1) | copy-start | bytes 393220
  1.5 0.8 %copy-start.2 = (f32[128,128]{1,0:T(8,128)S(1)}, f32[128,128]{1,0:T(8,128)}, u32[]{:S(2)}) copy-start(f32[128,128]{1,0:T(8,128)} %diag_ref.1) | copy-start | bytes 196612
  2.4 24.0 %copy-start = (f32[2048,256]{1,0:T(8,128)S(1)}, f32[2048,256]{1,0:T(8,128)}, u32[]{:S(2)}) copy-start(f32[2048,256]{1,0:T(8,128)} %refs_10_.1) | copy-start | bytes 6291460
  7.3 5.6 %collective-permute-start.1 = (bf16[256,128]{1,0:T(8,128)(2,1)S(1)}, bf16[256,128]{1,0:T(8,128)(2,1)S(1)}, u32[]{:S(2)}, u32[]{:S(2)}) collective-permute-start(bf16[256,128]{1,0:T(8,128)(2,1)S(1)} %get-tuple-element.4.refs_0_), channel_id=1, source_target_pairs={{0,2},{1,3},{2,0},{3,1},{4,6},{5,7},{6,4},{7,5},{8,10},{9,11},{10,... | collective-permute-start | bytes 196616 | tf_op jit(solution)/shard_map/ppermute | solution.py:205
  10.3 7.3 %collective-permute-start = (bf16[256,128]{1,0:T(8,128)(2,1)S(1)}, bf16[256,128]{1,0:T(8,128)(2,1)S(1)}, u32[]{:S(2)}, u32[]{:S(2)}) collective-permute-start(bf16[256,128]{1,0:T(8,128)(2,1)S(1)} %get-tuple-element.4.refs_0_), channel_id=1, source_target_pairs={{0,4},{1,5},{2,6},{3,7},{4,0},{5,1},{6,2},{7,3},{8,12},{9,13},{10,... | collective-permute-start | bytes 196616 | tf_op jit(solution)/shard_map/ppermute | solution.py:205
  12.9 8.2 %collective-permute-start.2 = (bf16[256,128]{1,0:T(8,128)(2,1)S(1)}, bf16[256,128]{1,0:T(8,128)(2,1)S(1)}, u32[]{:S(2)}, u32[]{:S(2)}) collective-permute-start(bf16[256,128]{1,0:T(8,128)(2,1)S(1)} %get-tuple-element.4.refs_0_), channel_id=1, source_target_pairs={{0,6},{1,7},{2,4},{3,5},{4,2},{5,3},{6,0},{7,1},{8,14},{9,15},{10,... | collective-permute-start | bytes 196616 | tf_op jit(solution)/shard_map/ppermute | solution.py:205
  17.6 4.1 %collective-permute-start.9 = (bf16[128,128]{1,0:T(8,128)(2,1)S(1)}, bf16[128,128]{1,0:T(8,128)(2,1)S(1)}, u32[]{:S(2)}, u32[]{:S(2)}) collective-permute-start(bf16[128,128]{1,0:T(8,128)(2,1)S(1)} %fusion), channel_id=1, source_target_pairs={{0,8},{8,0},{16,24},{24,16},{1,9},{9,1},{17,25},{25,17},{2,10},{10... | collective-permute-start | bytes 98312 | tf_op jit(solution)/shard_map/ppermute | solution.py:217
  19.1 3.9 %collective-permute-start.8 = (bf16[128,128]{1,0:T(8,128)(2,1)S(1)}, bf16[128,128]{1,0:T(8,128)(2,1)S(1)}, u32[]{:S(2)}, u32[]{:S(2)}) collective-permute-start(bf16[128,128]{1,0:T(8,128)(2,1)S(1)} %fusion), channel_id=1, source_target_pairs={{0,16},{8,24},{16,0},{24,8},{1,17},{9,25},{17,1},{25,9},{2,18},{10... | collective-permute-start | bytes 98312 | tf_op jit(solution)/shard_map/ppermute | solution.py:217
  20.3 4.8 %collective-permute-start.7 = (bf16[128,128]{1,0:T(8,128)(2,1)S(1)}, bf16[128,128]{1,0:T(8,128)(2,1)S(1)}, u32[]{:S(2)}, u32[]{:S(2)}) collective-permute-start(bf16[128,128]{1,0:T(8,128)(2,1)S(1)} %fusion), channel_id=1, source_target_pairs={{0,24},{8,16},{16,8},{24,0},{1,25},{9,17},{17,9},{25,1},{2,26},{10... | collective-permute-start | bytes 98312 | tf_op jit(solution)/shard_map/ppermute | solution.py:217
  21.1 4.0 %collective-permute-start.3 = (bf16[256,128]{1,0:T(8,128)(2,1)S(1)}, bf16[256,128]{1,0:T(8,128)(2,1)S(1)}, u32[]{:S(2)}, u32[]{:S(2)}) collective-permute-start(bf16[256,128]{1,0:T(8,128)(2,1)S(1)} %get-tuple-element.4.refs_0_), channel_id=1, source_target_pairs={{0,1},{1,0},{2,3},{3,2},{4,5},{5,4},{6,7},{7,6},{8,9},{9,8},{10,11... | collective-permute-start | bytes 196616 | tf_op jit(solution)/shard_map/ppermute | solution.py:219
  21.1 4.1 %collective-permute-start.5 = (bf16[256,128]{1,0:T(8,128)(2,1)S(1)}, bf16[256,128]{1,0:T(8,128)(2,1)S(1)}, u32[]{:S(2)}, u32[]{:S(2)}) collective-permute-start(bf16[256,128]{1,0:T(8,128)(2,1)S(1)} %collective-permute-done.1.refs_2_), channel_id=1, source_target_pairs={{0,1},{1,0},{2,3},{3,2},{4,5},{5,4},{6,7},{7,6},{8,9},{9,8},{10,11... | collective-permute-start | bytes 196616 | tf_op jit(solution)/shard_map/ppermute | solution.py:219
  21.7 4.7 %collective-permute-start.4 = (bf16[256,128]{1,0:T(8,128)(2,1)S(1)}, bf16[256,128]{1,0:T(8,128)(2,1)S(1)}, u32[]{:S(2)}, u32[]{:S(2)}) collective-permute-start(bf16[256,128]{1,0:T(8,128)(2,1)S(1)} %collective-permute-done.refs_1_), channel_id=1, source_target_pairs={{0,1},{1,0},{2,3},{3,2},{4,5},{5,4},{6,7},{7,6},{8,9},{9,8},{10,11... | collective-permute-start | bytes 196616 | tf_op jit(solution)/shard_map/ppermute | solution.py:219
  23.1 2.1 %collective-permute-start.6 = (bf16[256,128]{1,0:T(8,128)(2,1)S(1)}, bf16[256,128]{1,0:T(8,128)(2,1)S(1)}, u32[]{:S(2)}, u32[]{:S(2)}) collective-permute-start(bf16[256,128]{1,0:T(8,128)(2,1)S(1)} %collective-permute-done.2.refs_3_), channel_id=1, source_target_pairs={{0,1},{1,0},{2,3},{3,2},{4,5},{5,4},{6,7},{7,6},{8,9},{9,8},{10,11... | collective-permute-start | bytes 196616 | tf_op jit(solution)/shard_map/ppermute | solution.py:219
  25.1 1.3 %collective-permute-start.10 = (bf16[128,128]{1,0:T(8,128)(2,1)S(1)}, bf16[128,128]{1,0:T(8,128)(2,1)S(1)}, u32[]{:S(2)}, u32[]{:S(2)}) collective-permute-start(bf16[128,128]{1,0:T(8,128)(2,1)S(1)} %get-tuple-element.6), channel_id=1, source_target_pairs={{0,1},{1,0},{2,3},{3,2},{4,5},{5,4},{6,7},{7,6},{8,9},{9,8},{10,11... | collective-permute-start | bytes 98312 | tf_op jit(solution)/shard_map/ppermute | solution.py:221

commit v2 on v1

--- a/solution.py
+++ b/solution.py
@@ -9,59 +9,89 @@
 
 
 GROUP = 8
+LANES = 128
 EXACT = lax.Precision.HIGHEST
 NT = (((1,), (1,)), ((), ()))
 
 
 def invert_factor(diag_ref, out_ref):
     n = diag_ref.shape[0]
+    groups = n // GROUP
     lane = lax.broadcasted_iota(jnp.int32, (GROUP, n), 1)
     sub = lax.broadcasted_iota(jnp.int32, (GROUP, n), 0)
-    rows = [diag_ref[i : i + GROUP, :] for i in range(0, n, GROUP)]
-
-    def column(x, at):
-        return jnp.broadcast_to(x[:, at : at + 1], (GROUP, n))
+    rows = [diag_ref[i * GROUP : (i + 1) * GROUP, :] for i in range(groups)]
+    zero = jnp.where(lane >= n, rows[0], 0.0)
+
+    def columns(x, first):
+        return [jnp.broadcast_to(x[:, at : at + 1], (GROUP, n)) for at in range(first, first + GROUP)]
 
     def row(x, at):
         return jnp.broadcast_to(x[at : at + 1, :], (GROUP, n))
 
-    for b in range(n // GROUP):
+    cols = [c + zero for c in columns(rows[0], 0)]
+    for b in range(groups):
         first = b * GROUP
         inside = (lane >= first) & (lane < first + GROUP)
-        cols = [column(rows[b], first + j) for j in range(GROUP)]
         work = jnp.where(inside, jnp.where(lane - first == sub, 1.0, 0.0), rows[b])
         scale, scaled, cross = [], [], {}
+        follows = b + 1 < groups
+        if follows:
+            below = columns(rows[b + 1], first)
+            ahead = [c + zero for c in columns(rows[b + 1], first + GROUP)]
+            rest = jnp.where(inside, 0.0, rows[b + 1])
         for k in range(GROUP):
             scale.append(lax.rsqrt(row(cols[k], k)))
             scaled.append(row(work, k) * scale[k])
             if k < GROUP - 1:
-                factor = jnp.where(sub > k, cols[k] * scale[k], 0.0)
+                factor = jnp.where(sub > k, cols[k], 0.0) * scale[k]
                 for j in range(k + 1, GROUP):
                     cross[k, j] = row(cols[j], k) * scale[k]
                     cols[j] = cols[j] - factor * cross[k, j]
                 work = work - factor * scaled[k]
+            if follows:
+                factor = below[k] * scale[k]
+                for j in range(k + 1, GROUP):
+                    below[j] = below[j] - factor * cross[k, j]
+                rest = rest - factor * scaled[k]
+                for j in range(GROUP):
+                    ahead[j] = ahead[j] - factor * row(factor, j)
         done = scaled[0]
         for k in range(1, GROUP):
             done = jnp.where(sub == k, scaled[k], done)
         out_ref[first : first + GROUP, :] = jnp.where(lane <= sub + first, done, 0.0)
-        for i in range(b + 1, n // GROUP):
-            cols = [column(rows[i], first + j) for j in range(GROUP)]
+        if follows:
+            cols = ahead
+            rows[b + 1] = rest
+        for i in range(b + 2, groups):
+            below = columns(rows[i], first)
             rest = jnp.where(inside, 0.0, rows[i])
             for k in range(GROUP):
-                factor = cols[k] * scale[k]
+                factor = below[k] * scale[k]
                 for j in range(k + 1, GROUP):
-                    cols[j] = cols[j] - factor * cross[k, j]
+                    below[j] = below[j] - factor * cross[k, j]
                 rest = rest - factor * scaled[k]
             rows[i] = rest
 
 
-def solve_kernel(diag_ref, panel_ref, factored_ref, low_ref, inverse):
-    invert_factor(diag_ref, inverse)
+def inverse_factor(diag_block):
+    vmem = pl.BlockSpec(memory_space=pltpu.VMEM)
+    return pl.pallas_call(
+        invert_factor,
+        out_shape=jax.ShapeDtypeStruct(diag_block.shape, jnp.float32),
+        in_specs=[vmem],
+        out_specs=vmem,
+        cost_estimate=pl.CostEstimate(flops=2_000_000_000, bytes_accessed=8 * diag_block.size, transcendentals=0),
+        compiler_params=pltpu.CompilerParams(vmem_limit_bytes=2 << 20),
+        name="inverse_factor",
+    )(diag_block)
+
+
+def solve_kernel(inverse_ref, panel_ref, solved_ref, low_ref):
     solved = lax.dot_general(
-        panel_ref[...], inverse[...], NT, precision=EXACT, preferred_element_type=jnp.float32
+        panel_ref[...], inverse_ref[...], NT, precision=EXACT, preferred_element_type=jnp.float32
     )
-    factored_ref[...] = solved
     low_ref[...] = solved.astype(jnp.bfloat16)
+    solved_ref[...] = solved
 
 
 def solve_panel(diag_block, panel):
@@ -74,11 +104,10 @@
         ),
         in_specs=[vmem, vmem],
         out_specs=(vmem, vmem),
-        scratch_shapes=[pltpu.VMEM(diag_block.shape, jnp.float32)],
-        cost_estimate=pl.CostEstimate(flops=2_000_000_000, bytes_accessed=8 * panel.size, transcendentals=0),
+        cost_estimate=pl.CostEstimate(flops=200_000_000, bytes_accessed=8 * panel.size, transcendentals=0),
         compiler_params=pltpu.CompilerParams(vmem_limit_bytes=2 << 20),
         name="solve_panel",
-    )(diag_block, panel)
+    )(inverse_factor(diag_block), panel)
 
 
 class Plan:
@@ -137,47 +166,68 @@
     return chosen
 
 
-def update_kernel(plan, count, *refs):
+def update_kernel(plan, count, sides, aliased, *refs):
     x_refs, refs = refs[:count], refs[count:]
-    mine_ref, other_ref, slab_ref, next_ref, column, out_vmem, sems = refs
+    strip_refs, refs = refs[: len(sides)], refs[len(sides) :]
+    if aliased:
+        slab_ref, _, next_ref, column, out_vmem, sems = refs
+    else:
+        slab_ref, solved_ref, next_ref, factored_ref, column, out_vmem, sems = refs
+        factored_copy = pltpu.make_async_copy(solved_ref, factored_ref, sems.at[count])
+        factored_copy.start()
     row, me = lax.axis_index("prow"), lax.axis_index("pcol")
     parity = lax.rem(me, 2)
     step = plan.step
-    for s in range(plan.strips_each):
-        for ref, side in ((mine_ref, parity), (other_ref, 1 - parity)):
-            at = pl.multiple_of((2 * s + side) * step, step)
-            column[pl.ds(at, step), :] = ref[s * step : (s + 1) * step, :]
-    whole = column[...]
+    across = pl.ds(0, plan.total)
+    if len(sides) == 1:
+        across = pl.ds(pl.multiple_of((parity ^ sides[0]) * step, step), step)
+        whole = strip_refs[0][...]
+    else:
+        for s in range(plan.strips_each):
+            for ref, side in zip(strip_refs, sides):
+                at = pl.multiple_of((2 * s + (parity ^ side)) * step, step)
+                column[pl.ds(at, step), :] = ref[s * step : (s + 1) * step, :]
+        whole = column[...]
     flips = [pick([f[j] for f in plan.flips], row) for j in range(plan.slots)]
     copies = []
     for n, ref in enumerate(x_refs):
         from_column = me ^ flips[n % plan.slots] ^ (n // plan.slots)
         at = pl.ds(pl.multiple_of(from_column * plan.height, plan.height), plan.height)
         product = lax.dot_general(ref[...], whole, NT, preferred_element_type=jnp.float32)
-        out_vmem[at, :] = slab_ref[at, :] - product
-        copy = pltpu.make_async_copy(out_vmem.at[at, :], next_ref.at[at, :], sems.at[n])
+        out_vmem[at, :] = slab_ref[at, across] - product
+        copy = pltpu.make_async_copy(out_vmem.at[at, :], next_ref.at[at, across], sems.at[n])
         copy.start()
         copies.append(copy)
+    if not aliased:
+        copies.append(factored_copy)
     for copy in copies:
         copy.wait()
 
 
-def update(plan, solved, mine, other, slab):
-    vmem = pl.BlockSpec(memory_space=pltpu.VMEM)
+def update(plan, solved, strips, sides, slab, own, previous):
+    vmem, hbm = pl.BlockSpec(memory_space=pltpu.VMEM), pl.BlockSpec(memory_space=pltpu.HBM)
+    aliased = previous is not None
+    wide = plan.step * plan.strips_each * len(sides)
+    operands = [*solved, *strips, slab, previous if aliased else own]
+    outs, out_specs = [jax.ShapeDtypeStruct(slab.shape, jnp.float32)], [hbm]
+    if not aliased:
+        outs.append(jax.ShapeDtypeStruct(own.shape, jnp.float32))
+        out_specs.append(hbm)
     return pl.pallas_call(
-        functools.partial(update_kernel, plan, len(solved)),
-        out_shape=jax.ShapeDtypeStruct(slab.shape, jnp.float32),
-        in_specs=[vmem] * (len(solved) + 3),
-        out_specs=pl.BlockSpec(memory_space=pl.ANY),
+        functools.partial(update_kernel, plan, len(solved), sides, aliased),
+        out_shape=tuple(outs),
+        in_specs=[vmem] * (len(operands) - 1) + [hbm if aliased else vmem],
+        out_specs=tuple(out_specs),
         scratch_shapes=[
-            pltpu.VMEM((plan.total, mine.shape[1]), jnp.bfloat16),
-            pltpu.VMEM(slab.shape, jnp.float32),
-            pltpu.SemaphoreType.DMA((plan.pcols,)),
+            pltpu.VMEM((plan.total, own.shape[1]), jnp.bfloat16),
+            pltpu.VMEM((slab.shape[0], wide), jnp.float32),
+            pltpu.SemaphoreType.DMA((plan.pcols + 1,)),
         ],
+        input_output_aliases={len(operands) - 1: 0} if aliased else {},
         cost_estimate=pl.CostEstimate(flops=300_000_000, bytes_accessed=8 * slab.size, transcendentals=0),
         compiler_params=pltpu.CompilerParams(vmem_limit_bytes=8 << 20),
-        name="update",
-    )(*solved, mine, other, slab)
+        name="update_rest" if aliased else "update",
+    )(*operands)
 
 
 def choose(options, index):
@@ -199,7 +249,7 @@
     device = row * pcols + me
     both = ("prow", "pcol")
     partner = [(i, i ^ 1) for i in range(pcols)]
-    factored, low = solve_panel(diag_block, panel)
+    own, low = solve_panel(diag_block, panel)
     solved = [low]
     for j in range(1, plan.slots):
         solved.append(lax.ppermute(low, both, plan.pairs(j)))
@@ -219,7 +269,11 @@
         solved.append(lax.ppermute(solved[j], "pcol", partner))
     mine = choose(received, row ^ lax.rem(me, prows))
     other = lax.ppermute(choose(received, row ^ lax.rem(me ^ 1, prows)), "pcol", partner)
-    slab_next = update(plan, solved, mine, other, slab)
+    if plan.strips_each == 1 and plan.step % LANES == 0:
+        slab_next, factored = update(plan, solved, [mine], (0,), slab, own, None)
+        (slab_next,) = update(plan, solved, [other], (1,), slab, own, slab_next)
+    else:
+        slab_next, factored = update(plan, solved, [mine, other], (0, 1), slab, own, None)
     return slab_next, factored
 
 

time: 28.2 us -> 25.1 us (0.89)
  Pallas kernels: 6.5 us -> 5.32 us
  waiting for transfers between devices: 9.19 us -> 8.03 us
  local copies, waits for them, and re-layouts: 1.74 us -> 0.88 us
    pallas_call x1, Pallas kernels: 4.88 us -> 0.28 us  [solve_panel(): pl.pallas_call(solve_kernel, out_shape=(jax.ShapeDtypeStruct(panel.shape,...]
    pallas_call x1 -> x3, Pallas kernels: 1.63 us -> 5.04 us  [the longest x1 2.56 us: inverse_factor(): pl.pallas_call(invert_factor, out_shape=jax.ShapeDtypeStruct(diag_block.s...]
    ppermute x1, waiting for transfers between devices: 1.16 us -> 0.01 us  [per_device(): lax.ppermute(choose(received, row ^ lax.rem(me ^ 1, prows)), 'pcol', part...]
    unnamed x6, local copies, waits for them, and re-layouts: 1.74 us -> 0.88 us
  transfers between devices with their start and end apart: 11 -> 11, of which waited for: 4 -> 3; matrix products, arithmetic and copies ran while one was open for 0% -> 0% of each run, Pallas kernels for 0% -> 5%
where the time goes in v2:
time: 25.1 us; the launch traced here: 24.9 us
  starting transfers between devices  9.92 us (40%)
  waiting for transfers between devices  8.03 us (32%)
  Pallas kernels  5.32 us (21%)
  local copies, waits for them, and re-layouts  0.88 us (4%)
  between operations  0.75 us (3%)
    ppermute x3, starting transfers between devices, per_device(): solved.append(lax.ppermute(low, both, plan.pairs(j)))  5.71 us
    ppermute x3, waiting for transfers between devices, per_device(): solved.append(lax.ppermute(low, both, plan.pairs(j)))  4.67 us
    ppermute x3, starting transfers between devices, per_device(): lax.ppermute(passed, 'prow', [(i, i ^ k) for i in range(prows)])  3.55 us
    ppermute x3, waiting for transfers between devices, per_device(): lax.ppermute(passed, 'prow', [(i, i ^ k) for i in range(prows)])  3.35 us
    pallas_call x1, Pallas kernels, inverse_factor(): pl.pallas_call(invert_factor, out_shape=jax.ShapeDtypeStruct(diag_block.s...  2.56 us
    pallas_call x2, Pallas kernels, update(): pl.pallas_call(functools.partial(update_kernel, plan, len(solved), sides,...  2.48 us
    unnamed x6, local copies, waits for them, and re-layouts  0.88 us
    ppermute x4, starting transfers between devices, per_device(): solved.append(lax.ppermute(solved[j], 'pcol', partner))  0.58 us
  transfers between devices with their start and end apart: 11, of which 3 were waited for; matrix products, arithmetic and copies ran while one was open for 0% of the time, Pallas kernels for 5%

profile of v2, /device:TPU:0, one launch (start us, length us, event | category | flops | bytes accessed | tf_op | source)
XLA Modules:
  0.0 24.9 jit_solution(13666993640411745843)
XLA Ops:
  0.6 0.0 copy-start.1
  0.6 0.0 copy-start.2
  0.6 0.9 %copy-done.2 = f32[128,128]{1,0:T(8,128)S(1)} copy-done((f32[128,128]{1,0:T(8,128)S(1)}, f32[128,128]{1,0:T(8,128)}, u32[]{:S(2)}) %copy-start.2) | copy-done | bytes 65560
  1.5 0.0 copy-start
  1.5 2.6 %inverse_factor.1.inverse_ref = f32[128,128]{1,0:T(8,128)S(1)} custom-call(f32[128,128]{1,0:T(8,128)S(1)} %copy-done.2), custom_call_target="tpu_custom_call" | custom-call | flops 2000000000 | bytes 131072 | tf_op jit(solution)/shard_map/inverse_factor/pallas_call | solution.py:78
  4.1 0.0 copy-done.1
  4.1 0.3 %solve_panel.1 = (f32[256,128]{1,0:T(8,128)S(1)}, bf16[256,128]{1,0:T(8,128)(2,1)S(1)}) custom-call(f32[128,128]{1,0:T(8,128)S(1)} %inverse_factor.1.inverse_ref, f32[256,128]{1,0:T(8,128)S(1)} %copy-done.1), custom_call_target="tpu_custom_call" | custom-call | flops 200000000 | bytes 262144 | tf_op jit(solution)/shard_map/solve_panel/pallas_call | solution.py:99
  4.4 3.1 %collective-permute-start.1 = (bf16[256,128]{1,0:T(8,128)(2,1)S(1)}, bf16[256,128]{1,0:T(8,128)(2,1)S(1)}, u32[]{:S(2)}, u32[]{:S(2)}) collective-permute-start(bf16[256,128]{1,0:T(8,128)(2,1)S(1)} %get-tuple-element.6.refs_0_), channel_id=1, source_target_pairs={{0,2},{1,3},{2,0},{3,1},{4,6},{5,7},{6,4},{7,5},{8,10},{9,11},{10,... | collective-permute-start | bytes 196616 | tf_op jit(solution)/shard_map/ppermute | solution.py:255
  7.5 2.6 %collective-permute-start = (bf16[256,128]{1,0:T(8,128)(2,1)S(1)}, bf16[256,128]{1,0:T(8,128)(2,1)S(1)}, u32[]{:S(2)}, u32[]{:S(2)}) collective-permute-start(bf16[256,128]{1,0:T(8,128)(2,1)S(1)} %get-tuple-element.6.refs_0_), channel_id=1, source_target_pairs={{0,4},{1,5},{2,6},{3,7},{4,0},{5,1},{6,2},{7,3},{8,12},{9,13},{10,... | collective-permute-start | bytes 196616 | tf_op jit(solution)/shard_map/ppermute | solution.py:255
  10.1 0.0 collective-permute-start.2
  10.1 0.0 collective-permute-done.1.refs_2_
  10.1 4.7 %collective-permute-done.refs_1_ = bf16[256,128]{1,0:T(8,128)(2,1)S(1)} collective-permute-done((bf16[256,128]{1,0:T(8,128)(2,1)S(1)}, bf16[256,128]{1,0:T(8,128)(2,1)S(1)}, u32[]{:S(2)}, u32[]{:S(2)}) %collective-permute-start) | collective-permute-done | bytes 65568 | tf_op jit(solution)/shard_map/ppermute | solution.py:255
  14.8 1.6 %collective-permute-start.9 = (bf16[128,128]{1,0:T(8,128)(2,1)S(1)}, bf16[128,128]{1,0:T(8,128)(2,1)S(1)}, u32[]{:S(2)}, u32[]{:S(2)}) collective-permute-start(bf16[128,128]{1,0:T(8,128)(2,1)S(1)} %fusion), channel_id=1, source_target_pairs={{0,8},{8,0},{16,24},{24,16},{1,9},{9,1},{17,25},{25,17},{2,10},{10... | collective-permute-start | bytes 98312 | tf_op jit(solution)/shard_map/ppermute | solution.py:267
  16.3 1.1 %collective-permute-start.8 = (bf16[128,128]{1,0:T(8,128)(2,1)S(1)}, bf16[128,128]{1,0:T(8,128)(2,1)S(1)}, u32[]{:S(2)}, u32[]{:S(2)}) collective-permute-start(bf16[128,128]{1,0:T(8,128)(2,1)S(1)} %fusion), channel_id=1, source_target_pairs={{0,16},{8,24},{16,0},{24,8},{1,17},{9,25},{17,1},{25,9},{2,18},{10... | collective-permute-start | bytes 98312 | tf_op jit(solution)/shard_map/ppermute | solution.py:267
  17.5 0.9 %collective-permute-start.7 = (bf16[128,128]{1,0:T(8,128)(2,1)S(1)}, bf16[128,128]{1,0:T(8,128)(2,1)S(1)}, u32[]{:S(2)}, u32[]{:S(2)}) collective-permute-start(bf16[128,128]{1,0:T(8,128)(2,1)S(1)} %fusion), channel_id=1, source_target_pairs={{0,24},{8,16},{16,8},{24,0},{1,25},{9,17},{17,9},{25,1},{2,26},{10... | collective-permute-start | bytes 98312 | tf_op jit(solution)/shard_map/ppermute | solution.py:267
  18.3 0.0 collective-permute-start.3
  18.3 0.0 collective-permute-done.2.refs_3_
  18.3 0.5 %collective-permute-start.5 = (bf16[256,128]{1,0:T(8,128)(2,1)S(1)}, bf16[256,128]{1,0:T(8,128)(2,1)S(1)}, u32[]{:S(2)}, u32[]{:S(2)}) collective-permute-start(bf16[256,128]{1,0:T(8,128)(2,1)S(1)} %collective-permute-done.1.refs_2_), channel_id=1, source_target_pairs={{0,1},{1,0},{2,3},{3,2},{4,5},{5,4},{6,7},{7,6},{8,9},{9,8},{10,11... | collective-permute-start | bytes 196616 | tf_op jit(solution)/shard_map/ppermute | solution.py:269
  18.9 0.0 collective-permute-done.9
  18.9 0.1 collective-permute-start.4
  18.9 1.3 %collective-permute-done.8 = bf16[128,128]{1,0:T(8,128)(2,1)S(1)} collective-permute-done((bf16[128,128]{1,0:T(8,128)(2,1)S(1)}, bf16[128,128]{1,0:T(8,128)(2,1)S(1)}, u32[]{:S(2)}, u32[]{:S(2)}) %collective-permute-start.8) | collective-permute-done | bytes 32800 | tf_op jit(solution)/shard_map/ppermute | solution.py:267
  20.3 0.0 collective-permute-start.6
  20.3 2.0 %collective-permute-done.7 = bf16[128,128]{1,0:T(8,128)(2,1)S(1)} collective-permute-done((bf16[128,128]{1,0:T(8,128)(2,1)S(1)}, bf16[128,128]{1,0:T(8,128)(2,1)S(1)}, u32[]{:S(2)}, u32[]{:S(2)}) %collective-permute-start.7) | collective-permute-done | bytes 32800 | tf_op jit(solution)/shard_map/ppermute | solution.py:267
  22.3 0.1 collective-permute-start.10
  22.4 0.0 collective-permute-done.3.refs_4_
  22.4 0.0 collective-permute-done.6.refs_7_
  22.4 0.0 collective-permute-done.5.refs_6_
  22.4 0.0 collective-permute-done.4.refs_5_
  22.4 0.0 copy-done
  22.4 1.2 %update.1 = (f32[2048,256]{1,0:T(8,128)}, f32[256,128]{1,0:T(8,128)}) custom-call(bf16[256,128]{1,0:T(8,128)(2,1)S(1)} %get-tuple-element.6.refs_0_, bf16[256,128]{1,0:T(8,128)(2,1)S(1)} %collective-permute-done.refs_1_, bf16[256,128]{1,0:T(8,128)(2,1)S(1)} %collective-permute-done.1.refs_2_, bf16[256,128]{1,0:T(8,128)(2,1)S(1)} %collective-permute-done.2.refs_3_, ...), custom_call_target="tpu_custom_call" | custom-call | flops 300000000 | bytes 4194304 | tf_op jit(solution)/shard_map/update/pallas_call | solution.py:216
  23.7 0.0 collective-permute-done.10.refs_8_
  23.7 1.2 %update_rest.1 = f32[2048,256]{1,0:T(8,128)} custom-call(bf16[256,128]{1,0:T(8,128)(2,1)S(1)} %get-tuple-element.6.refs_0_, bf16[256,128]{1,0:T(8,128)(2,1)S(1)} %collective-permute-done.refs_1_, bf16[256,128]{1,0:T(8,128)(2,1)S(1)} %collective-permute-done.1.refs_2_, ...), custom_call_target="tpu_custom_call", output_to_operand_aliasing={{}: (10, {})} | custom-call | flops 300000000 | bytes 4194304 | tf_op jit(solution)/shard_map/update_rest/pallas_call | solution.py:216
  (2 shorter events, 0.0 us)
Async XLA Ops:
  0.6 3.5 %copy-start.1 = (f32[256,128]{1,0:T(8,128)S(1)}, f32[256,128]{1,0:T(8,128)}, u32[]{:S(2)}) copy-start(f32[256,128]{1,0:T(8,128)} %panel_ref.1) | copy-start | bytes 393220
  0.6 0.9 %copy-start.2 = (f32[128,128]{1,0:T(8,128)S(1)}, f32[128,128]{1,0:T(8,128)}, u32[]{:S(2)}) copy-start(f32[128,128]{1,0:T(8,128)} %diag_ref.1) | copy-start | bytes 196612
  1.5 20.9 %copy-start = (f32[2048,256]{1,0:T(8,128)S(1)}, f32[2048,256]{1,0:T(8,128)}, u32[]{:S(2)}) copy-start(f32[2048,256]{1,0:T(8,128)} %refs_9_.3) | copy-start | bytes 6291460
  4.4 5.7 %collective-permute-start.1 = (bf16[256,128]{1,0:T(8,128)(2,1)S(1)}, bf16[256,128]{1,0:T(8,128)(2,1)S(1)}, u32[]{:S(2)}, u32[]{:S(2)}) collective-permute-start(bf16[256,128]{1,0:T(8,128)(2,1)S(1)} %get-tuple-element.6.refs_0_), channel_id=1, source_target_pairs={{0,2},{1,3},{2,0},{3,1},{4,6},{5,7},{6,4},{7,5},{8,10},{9,11},{10,... | collective-permute-start | bytes 196616 | tf_op jit(solution)/shard_map/ppermute | solution.py:255
  7.5 7.3 %collective-permute-start = (bf16[256,128]{1,0:T(8,128)(2,1)S(1)}, bf16[256,128]{1,0:T(8,128)(2,1)S(1)}, u32[]{:S(2)}, u32[]{:S(2)}) collective-permute-start(bf16[256,128]{1,0:T(8,128)(2,1)S(1)} %get-tuple-element.6.refs_0_), channel_id=1, source_target_pairs={{0,4},{1,5},{2,6},{3,7},{4,0},{5,1},{6,2},{7,3},{8,12},{9,13},{10,... | collective-permute-start | bytes 196616 | tf_op jit(solution)/shard_map/ppermute | solution.py:255
  10.1 8.2 %collective-permute-start.2 = (bf16[256,128]{1,0:T(8,128)(2,1)S(1)}, bf16[256,128]{1,0:T(8,128)(2,1)S(1)}, u32[]{:S(2)}, u32[]{:S(2)}) collective-permute-start(bf16[256,128]{1,0:T(8,128)(2,1)S(1)} %get-tuple-element.6.refs_0_), channel_id=1, source_target_pairs={{0,6},{1,7},{2,4},{3,5},{4,2},{5,3},{6,0},{7,1},{8,14},{9,15},{10,... | collective-permute-start | bytes 196616 | tf_op jit(solution)/shard_map/ppermute | solution.py:255
  14.8 4.1 %collective-permute-start.9 = (bf16[128,128]{1,0:T(8,128)(2,1)S(1)}, bf16[128,128]{1,0:T(8,128)(2,1)S(1)}, u32[]{:S(2)}, u32[]{:S(2)}) collective-permute-start(bf16[128,128]{1,0:T(8,128)(2,1)S(1)} %fusion), channel_id=1, source_target_pairs={{0,8},{8,0},{16,24},{24,16},{1,9},{9,1},{17,25},{25,17},{2,10},{10... | collective-permute-start | bytes 98312 | tf_op jit(solution)/shard_map/ppermute | solution.py:267
  16.3 3.9 %collective-permute-start.8 = (bf16[128,128]{1,0:T(8,128)(2,1)S(1)}, bf16[128,128]{1,0:T(8,128)(2,1)S(1)}, u32[]{:S(2)}, u32[]{:S(2)}) collective-permute-start(bf16[128,128]{1,0:T(8,128)(2,1)S(1)} %fusion), channel_id=1, source_target_pairs={{0,16},{8,24},{16,0},{24,8},{1,17},{9,25},{17,1},{25,9},{2,18},{10... | collective-permute-start | bytes 98312 | tf_op jit(solution)/shard_map/ppermute | solution.py:267
  17.5 4.8 %collective-permute-start.7 = (bf16[128,128]{1,0:T(8,128)(2,1)S(1)}, bf16[128,128]{1,0:T(8,128)(2,1)S(1)}, u32[]{:S(2)}, u32[]{:S(2)}) collective-permute-start(bf16[128,128]{1,0:T(8,128)(2,1)S(1)} %fusion), channel_id=1, source_target_pairs={{0,24},{8,16},{16,8},{24,0},{1,25},{9,17},{17,9},{25,1},{2,26},{10... | collective-permute-start | bytes 98312 | tf_op jit(solution)/shard_map/ppermute | solution.py:267
  18.3 4.0 %collective-permute-start.3 = (bf16[256,128]{1,0:T(8,128)(2,1)S(1)}, bf16[256,128]{1,0:T(8,128)(2,1)S(1)}, u32[]{:S(2)}, u32[]{:S(2)}) collective-permute-start(bf16[256,128]{1,0:T(8,128)(2,1)S(1)} %get-tuple-element.6.refs_0_), channel_id=1, source_target_pairs={{0,1},{1,0},{2,3},{3,2},{4,5},{5,4},{6,7},{7,6},{8,9},{9,8},{10,11... | collective-permute-start | bytes 196616 | tf_op jit(solution)/shard_map/ppermute | solution.py:269
  18.3 4.1 %collective-permute-start.5 = (bf16[256,128]{1,0:T(8,128)(2,1)S(1)}, bf16[256,128]{1,0:T(8,128)(2,1)S(1)}, u32[]{:S(2)}, u32[]{:S(2)}) collective-permute-start(bf16[256,128]{1,0:T(8,128)(2,1)S(1)} %collective-permute-done.1.refs_2_), channel_id=1, source_target_pairs={{0,1},{1,0},{2,3},{3,2},{4,5},{5,4},{6,7},{7,6},{8,9},{9,8},{10,11... | collective-permute-start | bytes 196616 | tf_op jit(solution)/shard_map/ppermute | solution.py:269
  18.9 3.6 %collective-permute-start.4 = (bf16[256,128]{1,0:T(8,128)(2,1)S(1)}, bf16[256,128]{1,0:T(8,128)(2,1)S(1)}, u32[]{:S(2)}, u32[]{:S(2)}) collective-permute-start(bf16[256,128]{1,0:T(8,128)(2,1)S(1)} %collective-permute-done.refs_1_), channel_id=1, source_target_pairs={{0,1},{1,0},{2,3},{3,2},{4,5},{5,4},{6,7},{7,6},{8,9},{9,8},{10,11... | collective-permute-start | bytes 196616 | tf_op jit(solution)/shard_map/ppermute | solution.py:269
  20.3 2.1 %collective-permute-start.6 = (bf16[256,128]{1,0:T(8,128)(2,1)S(1)}, bf16[256,128]{1,0:T(8,128)(2,1)S(1)}, u32[]{:S(2)}, u32[]{:S(2)}) collective-permute-start(bf16[256,128]{1,0:T(8,128)(2,1)S(1)} %collective-permute-done.2.refs_3_), channel_id=1, source_target_pairs={{0,1},{1,0},{2,3},{3,2},{4,5},{5,4},{6,7},{7,6},{8,9},{9,8},{10,11... | collective-permute-start | bytes 196616 | tf_op jit(solution)/shard_map/ppermute | solution.py:269
  22.3 1.4 %collective-permute-start.10 = (bf16[128,128]{1,0:T(8,128)(2,1)S(1)}, bf16[128,128]{1,0:T(8,128)(2,1)S(1)}, u32[]{:S(2)}, u32[]{:S(2)}) collective-permute-start(bf16[128,128]{1,0:T(8,128)(2,1)S(1)} %get-tuple-element.11), channel_id=1, source_target_pairs={{0,1},{1,0},{2,3},{3,2},{4,5},{5,4},{6,7},{7,6},{8,9},{9,8},{10,11... | collective-permute-start | bytes 98312 | tf_op jit(solution)/shard_map/ppermute | solution.py:271

commit v3 on v2

--- a/solution.py
+++ b/solution.py
@@ -10,6 +10,7 @@
 
 GROUP = 8
 LANES = 128
+FAR = (-1, 0)
 EXACT = lax.Precision.HIGHEST
 NT = (((1,), (1,)), ((), ()))
 
@@ -73,41 +74,70 @@
             rows[i] = rest
 
 
-def inverse_factor(diag_block):
-    vmem = pl.BlockSpec(memory_space=pltpu.VMEM)
-    return pl.pallas_call(
-        invert_factor,
-        out_shape=jax.ShapeDtypeStruct(diag_block.shape, jnp.float32),
-        in_specs=[vmem],
-        out_specs=vmem,
-        cost_estimate=pl.CostEstimate(flops=2_000_000_000, bytes_accessed=8 * diag_block.size, transcendentals=0),
-        compiler_params=pltpu.CompilerParams(vmem_limit_bytes=2 << 20),
-        name="inverse_factor",
-    )(diag_block)
-
-
-def solve_kernel(inverse_ref, panel_ref, solved_ref, low_ref):
-    solved = lax.dot_general(
-        panel_ref[...], inverse_ref[...], NT, precision=EXACT, preferred_element_type=jnp.float32
-    )
+def only_for(devices, wanted, body):
+    me = lax.axis_index("pcol")
+    listed = functools.reduce(jnp.logical_or, [me == i for i in devices])
+    pl.when(listed if wanted else jnp.logical_not(listed))(body)
+
+
+def solve_rows(inverse_ref, rows, solved_ref, low_ref):
+    solved = lax.dot_general(rows[...], inverse_ref[...], NT, precision=EXACT, preferred_element_type=jnp.float32)
     low_ref[...] = solved.astype(jnp.bfloat16)
     solved_ref[...] = solved
 
 
-def solve_panel(diag_block, panel):
-    vmem = pl.BlockSpec(memory_space=pltpu.VMEM)
+def first_kernel(devices, diag_hbm, panel_hbm, solved_ref, low_ref, diag, panel, inverse, sems):
+    def body():
+        diag_copy = pltpu.make_async_copy(diag_hbm, diag, sems.at[0])
+        panel_copy = pltpu.make_async_copy(panel_hbm, panel, sems.at[1])
+        diag_copy.start()
+        panel_copy.start()
+        diag_copy.wait()
+        invert_factor(diag, inverse)
+        panel_copy.wait()
+        solve_rows(inverse, panel, solved_ref, low_ref)
+
+    only_for(devices, True, body)
+
+
+def rest_kernel(devices, panel_hbm, diag_ref, _, __, solved_ref, low_ref, panel, inverse, sems):
+    def body():
+        panel_copy = pltpu.make_async_copy(panel_hbm, panel, sems.at[0])
+        panel_copy.start()
+        invert_factor(diag_ref, inverse)
+        panel_copy.wait()
+        solve_rows(inverse, panel, solved_ref, low_ref)
+
+    only_for(devices, False, body)
+
+
+def solve_panel(diag_block, panel, devices, before):
+    vmem, hbm = pl.BlockSpec(memory_space=pltpu.VMEM), pl.BlockSpec(memory_space=pl.ANY)
+    panel_hbm = pltpu.with_memory_space_constraint(panel, pltpu.HBM)
+    if before:
+        operands, in_specs = (panel_hbm, diag_block, *before), [hbm, vmem, vmem, vmem]
+    else:
+        operands = (pltpu.with_memory_space_constraint(diag_block, pltpu.HBM), panel_hbm)
+        in_specs = [hbm, hbm]
     return pl.pallas_call(
-        solve_kernel,
+        functools.partial(rest_kernel if before else first_kernel, devices),
         out_shape=(
             jax.ShapeDtypeStruct(panel.shape, jnp.float32),
             jax.ShapeDtypeStruct(panel.shape, jnp.bfloat16),
         ),
-        in_specs=[vmem, vmem],
+        in_specs=in_specs,
         out_specs=(vmem, vmem),
-        cost_estimate=pl.CostEstimate(flops=200_000_000, bytes_accessed=8 * panel.size, transcendentals=0),
+        scratch_shapes=([] if before else [pltpu.VMEM(diag_block.shape, jnp.float32)])
+        + [
+            pltpu.VMEM(panel.shape, jnp.float32),
+            pltpu.VMEM(diag_block.shape, jnp.float32),
+            pltpu.SemaphoreType.DMA((2,)),
+        ],
+        input_output_aliases={2: 0, 3: 1} if before else {},
+        cost_estimate=pl.CostEstimate(flops=2_000_000_000, bytes_accessed=8 * panel.size, transcendentals=0),
         compiler_params=pltpu.CompilerParams(vmem_limit_bytes=2 << 20),
-        name="solve_panel",
-    )(inverse_factor(diag_block), panel)
+        name="solve_rest" if before else "solve_first",
+    )(*operands)
 
 
 class Plan:
@@ -130,26 +160,52 @@
         assert parity == [s % 2 for s in range(len(parity))]
         self.strips_each = len(parity) // 2
         self.slots = pcols // 2
+        self.far = {}
+        if self.strips_each == 1:
+            for row in range(min(prows, pcols)):
+                column = max(range(row, pcols, prows))
+                (even, at), (odd, same) = strips(column)
+                if at == same and even // 2 == odd // 2 != column // 2:
+                    self.far[row] = (column, even // 2, at)
+        if len(self.far) < prows or len({at for _, _, at in self.far.values()}) > 1:
+            self.far = {}
+        self.sources = sorted({2 * chip + t for _, chip, _ in self.far.values() for t in range(2)})
+        if not self.far:
+            self.sources = range(pcols)
         self.flips = []
         for row in range(prows):
             first = []
             for column in range(row, pcols, prows):
+                if self.far and column == self.far[row][0]:
+                    continue
                 for shard, _ in strips(column):
                     k = 2 * ((shard // 2) ^ (column // 2))
                     if k and k not in first:
                         first.append(k)
             first.sort(reverse=True)
-            rest = [k for k in range(2, pcols, 2) if k not in first]
+            rest = [k for k in range(pcols - 2, 0, -2) if k not in first]
+            if self.far and not first:
+                first, rest = rest[-1:], rest[:-1]
             self.flips.append([0] + first + rest)
         self.places = [[None] * (prows * pcols) for _ in range(self.strips_each)]
         for row in range(prows):
             for me in range(pcols):
                 for column in (me, me ^ 1):
                     if column % prows == row:
+                        if self.far and column == self.far[row][0]:
+                            self.places[0][row * pcols + me] = FAR
+                            continue
                         own = [s for s in strips(column) if s[0] % 2 == me % 2]
                         for n, (shard, at) in enumerate(own):
                             slot = self.flips[row].index(2 * ((shard // 2) ^ (me // 2)))
                             self.places[n][row * pcols + me] = (slot, at)
+
+    def far_pairs(self):
+        return [
+            (row * self.pcols + 2 * chip + t, row * self.pcols + (column // 2) * 2 + t)
+            for row, (column, chip, _) in self.far.items()
+            for t in range(2)
+        ]
 
     def pairs(self, slot):
         return [
@@ -249,7 +305,11 @@
     device = row * pcols + me
     both = ("prow", "pcol")
     partner = [(i, i ^ 1) for i in range(pcols)]
-    own, low = solve_panel(diag_block, panel)
+    own, low = solve_panel(diag_block, panel, plan.sources, ())
+    if plan.far:
+        at = plan.far[0][2]
+        far = lax.ppermute(low[at : at + plan.step], both, plan.far_pairs())
+        own, low = solve_panel(diag_block, panel, plan.sources, (own, low))
     solved = [low]
     for j in range(1, plan.slots):
         solved.append(lax.ppermute(low, both, plan.pairs(j)))
@@ -260,7 +320,12 @@
         for at, place in enumerate(places):
             if place is not None:
                 options.setdefault(place, []).append(at)
-        strips.append(choose([(solved[j][at : at + plan.step], where) for (j, at), where in options.items()], device))
+        strips.append(
+            choose(
+                [(far if j < 0 else solved[j][at : at + plan.step], where) for (j, at), where in options.items()],
+                device,
+            )
+        )
     passed = jnp.concatenate(strips, 0) if len(strips) > 1 else strips[0]
     received = [(passed, [0])]
     for k in range(1, prows):

time: 25.1 us -> 24.3 us (0.968)
  waiting for transfers between devices: 8.03 us -> 5.09 us
  starting transfers between devices: 9.92 us -> 11.9 us
  Pallas kernels: 5.32 us -> 6.29 us
  local copies, waits for them, and re-layouts: 0.88 us -> 0.01 us
    ppermute x0 -> x1, starting transfers between devices: none -> 4.48 us  [per_device(): far = lax.ppermute(low[at:at + plan.step], both, plan.far_pairs())]
    ppermute x3, waiting for transfers between devices: 4.67 us -> 1.02 us  [per_device(): solved.append(lax.ppermute(low, both, plan.pairs(j)))]
    ppermute x3, starting transfers between devices: 5.71 us -> 3.11 us  [per_device(): solved.append(lax.ppermute(low, both, plan.pairs(j)))]
    ppermute x0 -> x1, waiting for transfers between devices: none -> 1.56 us  [per_device(): far = lax.ppermute(low[at:at + plan.step], both, plan.far_pairs())]
    pallas_call x2, Pallas kernels: 2.85 us -> 3.81 us  [solve_panel(): pl.pallas_call(functools.partial(rest_kernel if before else first_kernel,...]
    unnamed x6 -> x4, local copies, waits for them, and re-layouts: 0.88 us -> 0.01 us
    ppermute x3, waiting for transfers between devices: 3.35 us -> 2.5 us  [per_device(): lax.ppermute(passed, 'prow', [(i, i ^ k) for i in range(prows)])]
  transfers between devices with their start and end apart: 11 -> 12, of which waited for: 3 -> 4; matrix products, arithmetic and copies ran while one was open for 0% -> 0% of each run, Pallas kernels for 5% -> 5%
where the time goes in v3:
time: 24.3 us; the launch traced here: 24.2 us
  starting transfers between devices  11.9 us (49%)
  Pallas kernels  6.29 us (26%)
  waiting for transfers between devices  5.09 us (21%)
  between operations  0.82 us (3%)
    ppermute x1, starting transfers between devices, per_device(): far = lax.ppermute(low[at:at + plan.step], both, plan.far_pairs())  4.48 us
    pallas_call x2, Pallas kernels, solve_panel(): pl.pallas_call(functools.partial(rest_kernel if before else first_kernel,...  3.81 us
    ppermute x3, starting transfers between devices, per_device(): lax.ppermute(passed, 'prow', [(i, i ^ k) for i in range(prows)])  3.55 us
    ppermute x3, starting transfers between devices, per_device(): solved.append(lax.ppermute(low, both, plan.pairs(j)))  3.11 us
    ppermute x3, waiting for transfers between devices, per_device(): lax.ppermute(passed, 'prow', [(i, i ^ k) for i in range(prows)])  2.5 us
    pallas_call x2, Pallas kernels, update(): pl.pallas_call(functools.partial(update_kernel, plan, len(solved), sides,...  2.48 us
    ppermute x1, waiting for transfers between devices, per_device(): far = lax.ppermute(low[at:at + plan.step], both, plan.far_pairs())  1.56 us
    ppermute x3, waiting for transfers between devices, per_device(): solved.append(lax.ppermute(low, both, plan.pairs(j)))  1.02 us
  transfers between devices with their start and end apart: 12, of which 4 were waited for; matrix products, arithmetic and copies ran while one was open for 0% of the time, Pallas kernels for 5%

profile of v3, /device:TPU:0, one launch (start us, length us, event | category | flops | bytes accessed | tf_op | source)
XLA Modules:
  0.0 24.2 jit_solution(7739166486697735706)
XLA Ops:
  0.6 0.0 copy-start.1
  0.6 3.8 %solve_first.1 = (f32[256,128]{1,0:T(8,128)S(1)}, bf16[256,128]{1,0:T(8,128)(2,1)S(1)}) custom-call(f32[128,128]{1,0:T(8,128)} %diag_ref.1, f32[256,128]{1,0:T(8,128)} %panel_hbm.3), custom_call_target="tpu_custom_call" | custom-call | flops 2000000000 | bytes 262144 | tf_op jit(solution)/shard_map/solve_first/pallas_call | solution.py:122
  4.4 0.0 copy-done.1
  4.5 0.0 copy-start
  4.5 3.0 %collective-permute-start = (bf16[256,128]{1,0:T(8,128)(2,1)S(1)}, bf16[256,128]{1,0:T(8,128)(2,1)S(1)}, u32[]{:S(2)}, u32[]{:S(2)}) collective-permute-start(bf16[256,128]{1,0:T(8,128)(2,1)S(1)} %get-tuple-element.10.refs_0_), channel_id=1, source_target_pairs={{0,2},{1,3},{2,0},{3,1},{4,6},{5,7},{6,4},{7,5},{8,10},{9,11},{10,... | collective-permute-start | bytes 196616 | tf_op jit(solution)/shard_map/ppermute | solution.py:315
  7.5 4.5 %collective-permute-start.7 = (bf16[128,128]{1,0:T(8,128)(2,1)S(1)}, bf16[128,128]{1,0:T(8,128)(2,1)S(1)}, u32[]{:S(2)}, u32[]{:S(2)}) collective-permute-start(bf16[128,128]{1,0:T(8,128)(2,1)S(1)} %slice.10), channel_id=1, source_target_pairs={{0,4},{1,5},{8,12},{9,13},{16,22},{17,23},{24,30},{25,31}} | collective-permute-start | bytes 98312 | tf_op jit(solution)/shard_map/ppermute | solution.py:311
  12.0 0.1 collective-permute-start.2
  12.0 0.1 collective-permute-start.1
  12.2 1.6 %collective-permute-done.7 = bf16[128,128]{1,0:T(8,128)(2,1)S(1)} collective-permute-done((bf16[128,128]{1,0:T(8,128)(2,1)S(1)}, bf16[128,128]{1,0:T(8,128)(2,1)S(1)}, u32[]{:S(2)}, u32[]{:S(2)}) %collective-permute-start.7) | collective-permute-done | bytes 32800 | tf_op jit(solution)/shard_map/ppermute | solution.py:311
  13.7 0.0 collective-permute-done.refs_1_
  13.7 1.6 %collective-permute-start.10 = (bf16[128,128]{1,0:T(8,128)(2,1)S(1)}, bf16[128,128]{1,0:T(8,128)(2,1)S(1)}, u32[]{:S(2)}, u32[]{:S(2)}) collective-permute-start(bf16[128,128]{1,0:T(8,128)(2,1)S(1)} %slice_select_fusion), channel_id=1, source_target_pairs={{0,8},{8,0},{16,24},{24,16},{1,9},{9,1},{17,25},{25,17},{2,10},{10... | collective-permute-start | bytes 98312 | tf_op jit(solution)/shard_map/ppermute | solution.py:332
  15.3 1.4 %collective-permute-start.9 = (bf16[128,128]{1,0:T(8,128)(2,1)S(1)}, bf16[128,128]{1,0:T(8,128)(2,1)S(1)}, u32[]{:S(2)}, u32[]{:S(2)}) collective-permute-start(bf16[128,128]{1,0:T(8,128)(2,1)S(1)} %slice_select_fusion), channel_id=1, source_target_pairs={{0,16},{8,24},{16,0},{24,8},{1,17},{9,25},{17,1},{25,9},{2,18},{10... | collective-permute-start | bytes 98312 | tf_op jit(solution)/shard_map/ppermute | solution.py:332
  16.7 0.6 %collective-permute-start.8 = (bf16[128,128]{1,0:T(8,128)(2,1)S(1)}, bf16[128,128]{1,0:T(8,128)(2,1)S(1)}, u32[]{:S(2)}, u32[]{:S(2)}) collective-permute-start(bf16[128,128]{1,0:T(8,128)(2,1)S(1)} %slice_select_fusion), channel_id=1, source_target_pairs={{0,24},{8,16},{16,8},{24,0},{1,25},{9,17},{17,9},{25,1},{2,26},{10... | collective-permute-start | bytes 98312 | tf_op jit(solution)/shard_map/ppermute | solution.py:332
  17.3 1.0 %collective-permute-done.2.refs_3_ = bf16[256,128]{1,0:T(8,128)(2,1)S(1)} collective-permute-done((bf16[256,128]{1,0:T(8,128)(2,1)S(1)}, bf16[256,128]{1,0:T(8,128)(2,1)S(1)}, u32[]{:S(2)}, u32[]{:S(2)}) %collective-permute-start.2) | collective-permute-done | bytes 65568 | tf_op jit(solution)/shard_map/ppermute | solution.py:315
  18.3 0.0 collective-permute-start.3
  18.3 0.0 collective-permute-done.1.refs_2_
  18.3 0.5 %collective-permute-start.4 = (bf16[256,128]{1,0:T(8,128)(2,1)S(1)}, bf16[256,128]{1,0:T(8,128)(2,1)S(1)}, u32[]{:S(2)}, u32[]{:S(2)}) collective-permute-start(bf16[256,128]{1,0:T(8,128)(2,1)S(1)} %collective-permute-done.refs_1_), channel_id=1, source_target_pairs={{0,1},{1,0},{2,3},{3,2},{4,5},{5,4},{6,7},{7,6},{8,9},{9,8},{10,11... | collective-permute-start | bytes 196616 | tf_op jit(solution)/shard_map/ppermute | solution.py:334
  18.8 0.0 collective-permute-done.10
  18.8 0.1 collective-permute-start.6
  18.9 0.3 %collective-permute-done.9 = bf16[128,128]{1,0:T(8,128)(2,1)S(1)} collective-permute-done((bf16[128,128]{1,0:T(8,128)(2,1)S(1)}, bf16[128,128]{1,0:T(8,128)(2,1)S(1)}, u32[]{:S(2)}, u32[]{:S(2)}) %collective-permute-start.9) | collective-permute-done | bytes 32800 | tf_op jit(solution)/shard_map/ppermute | solution.py:332
  19.2 0.1 collective-permute-start.5
  19.3 2.2 %collective-permute-done.8 = bf16[128,128]{1,0:T(8,128)(2,1)S(1)} collective-permute-done((bf16[128,128]{1,0:T(8,128)(2,1)S(1)}, bf16[128,128]{1,0:T(8,128)(2,1)S(1)}, u32[]{:S(2)}, u32[]{:S(2)}) %collective-permute-start.8) | collective-permute-done | bytes 32800 | tf_op jit(solution)/shard_map/ppermute | solution.py:332
  21.5 0.1 collective-permute-start.11
  21.6 0.0 collective-permute-done.3.refs_4_
  21.6 0.0 collective-permute-done.6.refs_7_
  21.6 0.0 collective-permute-done.5.refs_6_
  21.6 0.0 collective-permute-done.4.refs_5_
  21.7 0.0 copy-done
  21.7 1.2 %update.1 = (f32[2048,256]{1,0:T(8,128)}, f32[256,128]{1,0:T(8,128)}) custom-call(bf16[256,128]{1,0:T(8,128)(2,1)S(1)} %get-tuple-element.10.refs_0_, bf16[256,128]{1,0:T(8,128)(2,1)S(1)} %collective-permute-done.refs_1_, bf16[256,128]{1,0:T(8,128)(2,1)S(1)} %collective-permute-done.1.refs_2_, bf16[256,128]{1,0:T(8,128)(2,1)S(1)} %collective-permute-done.2.refs_3_, ...), custom_call_target="tpu_custom_call" | custom-call | flops 300000000 | bytes 4194304 | tf_op jit(solution)/shard_map/update/pallas_call | solution.py:272
  22.9 0.0 collective-permute-done.11.refs_8_
  22.9 1.2 %update_rest.1 = f32[2048,256]{1,0:T(8,128)} custom-call(bf16[256,128]{1,0:T(8,128)(2,1)S(1)} %get-tuple-element.10.refs_0_, bf16[256,128]{1,0:T(8,128)(2,1)S(1)} %collective-permute-done.refs_1_, bf16[256,128]{1,0:T(8,128)(2,1)S(1)} %collective-permute-done.1.refs_2_, ...), custom_call_target="tpu_custom_call", output_to_operand_aliasing={{}: (10, {})} | custom-call | flops 300000000 | bytes 4194304 | tf_op jit(solution)/shard_map/update_rest/pallas_call | solution.py:272
  (4 shorter events, 0.1 us)
Async XLA Ops:
  0.6 3.8 %copy-start.1 = (f32[128,128]{1,0:T(8,128)S(1)}, f32[128,128]{1,0:T(8,128)}, u32[]{:S(2)}) copy-start(f32[128,128]{1,0:T(8,128)} %diag_ref.1) | copy-start | bytes 196612
  4.5 17.2 %copy-start = (f32[2048,256]{1,0:T(8,128)S(1)}, f32[2048,256]{1,0:T(8,128)}, u32[]{:S(2)}) copy-start(f32[2048,256]{1,0:T(8,128)} %refs_9_.3) | copy-start | bytes 6291460
  4.5 9.2 %collective-permute-start = (bf16[256,128]{1,0:T(8,128)(2,1)S(1)}, bf16[256,128]{1,0:T(8,128)(2,1)S(1)}, u32[]{:S(2)}, u32[]{:S(2)}) collective-permute-start(bf16[256,128]{1,0:T(8,128)(2,1)S(1)} %get-tuple-element.10.refs_0_), channel_id=1, source_target_pairs={{0,2},{1,3},{2,0},{3,1},{4,6},{5,7},{6,4},{7,5},{8,10},{9,11},{10,... | collective-permute-start | bytes 196616 | tf_op jit(solution)/shard_map/ppermute | solution.py:315
  7.5 6.2 %collective-permute-start.7 = (bf16[128,128]{1,0:T(8,128)(2,1)S(1)}, bf16[128,128]{1,0:T(8,128)(2,1)S(1)}, u32[]{:S(2)}, u32[]{:S(2)}) collective-permute-start(bf16[128,128]{1,0:T(8,128)(2,1)S(1)} %slice.10), channel_id=1, source_target_pairs={{0,4},{1,5},{8,12},{9,13},{16,22},{17,23},{24,30},{25,31}} | collective-permute-start | bytes 98312 | tf_op jit(solution)/shard_map/ppermute | solution.py:311
  12.0 6.3 %collective-permute-start.2 = (bf16[256,128]{1,0:T(8,128)(2,1)S(1)}, bf16[256,128]{1,0:T(8,128)(2,1)S(1)}, u32[]{:S(2)}, u32[]{:S(2)}) collective-permute-start(bf16[256,128]{1,0:T(8,128)(2,1)S(1)} %get-tuple-element.10.refs_0_), channel_id=1, source_target_pairs={{0,4},{1,5},{2,6},{3,7},{4,0},{5,1},{6,2},{7,3},{8,12},{9,13},{10,... | collective-permute-start | bytes 196616 | tf_op jit(solution)/shard_map/ppermute | solution.py:315
  12.0 6.3 %collective-permute-start.1 = (bf16[256,128]{1,0:T(8,128)(2,1)S(1)}, bf16[256,128]{1,0:T(8,128)(2,1)S(1)}, u32[]{:S(2)}, u32[]{:S(2)}) collective-permute-start(bf16[256,128]{1,0:T(8,128)(2,1)S(1)} %get-tuple-element.10.refs_0_), channel_id=1, source_target_pairs={{0,6},{1,7},{2,4},{3,5},{4,2},{5,3},{6,0},{7,1},{8,14},{9,15},{10,... | collective-permute-start | bytes 196616 | tf_op jit(solution)/shard_map/ppermute | solution.py:315
  13.7 5.1 %collective-permute-start.10 = (bf16[128,128]{1,0:T(8,128)(2,1)S(1)}, bf16[128,128]{1,0:T(8,128)(2,1)S(1)}, u32[]{:S(2)}, u32[]{:S(2)}) collective-permute-start(bf16[128,128]{1,0:T(8,128)(2,1)S(1)} %slice_select_fusion), channel_id=1, source_target_pairs={{0,8},{8,0},{16,24},{24,16},{1,9},{9,1},{17,25},{25,17},{2,10},{10... | collective-permute-start | bytes 98312 | tf_op jit(solution)/shard_map/ppermute | solution.py:332
  15.3 3.9 %collective-permute-start.9 = (bf16[128,128]{1,0:T(8,128)(2,1)S(1)}, bf16[128,128]{1,0:T(8,128)(2,1)S(1)}, u32[]{:S(2)}, u32[]{:S(2)}) collective-permute-start(bf16[128,128]{1,0:T(8,128)(2,1)S(1)} %slice_select_fusion), channel_id=1, source_target_pairs={{0,16},{8,24},{16,0},{24,8},{1,17},{9,25},{17,1},{25,9},{2,18},{10... | collective-permute-start | bytes 98312 | tf_op jit(solution)/shard_map/ppermute | solution.py:332
  16.7 4.8 %collective-permute-start.8 = (bf16[128,128]{1,0:T(8,128)(2,1)S(1)}, bf16[128,128]{1,0:T(8,128)(2,1)S(1)}, u32[]{:S(2)}, u32[]{:S(2)}) collective-permute-start(bf16[128,128]{1,0:T(8,128)(2,1)S(1)} %slice_select_fusion), channel_id=1, source_target_pairs={{0,24},{8,16},{16,8},{24,0},{1,25},{9,17},{17,9},{25,1},{2,26},{10... | collective-permute-start | bytes 98312 | tf_op jit(solution)/shard_map/ppermute | solution.py:332
  18.3 3.3 %collective-permute-start.3 = (bf16[256,128]{1,0:T(8,128)(2,1)S(1)}, bf16[256,128]{1,0:T(8,128)(2,1)S(1)}, u32[]{:S(2)}, u32[]{:S(2)}) collective-permute-start(bf16[256,128]{1,0:T(8,128)(2,1)S(1)} %get-tuple-element.10.refs_0_), channel_id=1, source_target_pairs={{0,1},{1,0},{2,3},{3,2},{4,5},{5,4},{6,7},{7,6},{8,9},{9,8},{10,11... | collective-permute-start | bytes 196616 | tf_op jit(solution)/shard_map/ppermute | solution.py:334
  18.3 3.3 %collective-permute-start.4 = (bf16[256,128]{1,0:T(8,128)(2,1)S(1)}, bf16[256,128]{1,0:T(8,128)(2,1)S(1)}, u32[]{:S(2)}, u32[]{:S(2)}) collective-permute-start(bf16[256,128]{1,0:T(8,128)(2,1)S(1)} %collective-permute-done.refs_1_), channel_id=1, source_target_pairs={{0,1},{1,0},{2,3},{3,2},{4,5},{5,4},{6,7},{7,6},{8,9},{9,8},{10,11... | collective-permute-start | bytes 196616 | tf_op jit(solution)/shard_map/ppermute | solution.py:334
  18.8 2.8 %collective-permute-start.6 = (bf16[256,128]{1,0:T(8,128)(2,1)S(1)}, bf16[256,128]{1,0:T(8,128)(2,1)S(1)}, u32[]{:S(2)}, u32[]{:S(2)}) collective-permute-start(bf16[256,128]{1,0:T(8,128)(2,1)S(1)} %collective-permute-done.2.refs_3_), channel_id=1, source_target_pairs={{0,1},{1,0},{2,3},{3,2},{4,5},{5,4},{6,7},{7,6},{8,9},{9,8},{10,11... | collective-permute-start | bytes 196616 | tf_op jit(solution)/shard_map/ppermute | solution.py:334
  19.2 2.4 %collective-permute-start.5 = (bf16[256,128]{1,0:T(8,128)(2,1)S(1)}, bf16[256,128]{1,0:T(8,128)(2,1)S(1)}, u32[]{:S(2)}, u32[]{:S(2)}) collective-permute-start(bf16[256,128]{1,0:T(8,128)(2,1)S(1)} %collective-permute-done.1.refs_2_), channel_id=1, source_target_pairs={{0,1},{1,0},{2,3},{3,2},{4,5},{5,4},{6,7},{7,6},{8,9},{9,8},{10,11... | collective-permute-start | bytes 196616 | tf_op jit(solution)/shard_map/ppermute | solution.py:334
  21.5 1.4 %collective-permute-start.11 = (bf16[128,128]{1,0:T(8,128)(2,1)S(1)}, bf16[128,128]{1,0:T(8,128)(2,1)S(1)}, u32[]{:S(2)}, u32[]{:S(2)}) collective-permute-start(bf16[128,128]{1,0:T(8,128)(2,1)S(1)} %get-tuple-element.15), channel_id=1, source_target_pairs={{0,1},{1,0},{2,3},{3,2},{4,5},{5,4},{6,7},{7,6},{8,9},{9,8},{10,11... | collective-permute-start | bytes 98312 | tf_op jit(solution)/shard_map/ppermute | solution.py:336

commit v4 on v3

--- a/solution.py
+++ b/solution.py
@@ -86,58 +86,74 @@
     solved_ref[...] = solved
 
 
-def first_kernel(devices, diag_hbm, panel_hbm, solved_ref, low_ref, diag, panel, inverse, sems):
+def panel_kernel(devices, first, panel_hbm, diag_ref, _, *refs):
+    inverse, solved_ref, low_ref, panel, sem = refs[-5:]
+
     def body():
-        diag_copy = pltpu.make_async_copy(diag_hbm, diag, sems.at[0])
-        panel_copy = pltpu.make_async_copy(panel_hbm, panel, sems.at[1])
-        diag_copy.start()
-        panel_copy.start()
-        diag_copy.wait()
-        invert_factor(diag, inverse)
-        panel_copy.wait()
-        solve_rows(inverse, panel, solved_ref, low_ref)
-
-    only_for(devices, True, body)
-
-
-def rest_kernel(devices, panel_hbm, diag_ref, _, __, solved_ref, low_ref, panel, inverse, sems):
-    def body():
-        panel_copy = pltpu.make_async_copy(panel_hbm, panel, sems.at[0])
+        panel_copy = pltpu.make_async_copy(panel_hbm, panel, sem)
         panel_copy.start()
         invert_factor(diag_ref, inverse)
         panel_copy.wait()
         solve_rows(inverse, panel, solved_ref, low_ref)
 
-    only_for(devices, False, body)
-
-
-def solve_panel(diag_block, panel, devices, before):
+    only_for(devices, first, body)
+
+
+def mark_kernel(*refs):
+    refs[-1][...] = jnp.zeros_like(refs[-1])
+
+
+def mark(*before):
+    vmem = pl.BlockSpec(memory_space=pltpu.VMEM)
+    return pl.pallas_call(
+        mark_kernel,
+        out_shape=jax.ShapeDtypeStruct((GROUP, LANES), jnp.float32),
+        in_specs=[vmem] * len(before),
+        out_specs=vmem,
+        cost_estimate=pl.CostEstimate(flops=400_000_000, bytes_accessed=4 * GROUP * LANES, transcendentals=0),
+        compiler_params=pltpu.CompilerParams(vmem_limit_bytes=2 << 20),
+        name="mark",
+    )(*before)
+
+
+def near_kernel(inverse_ref, rows_ref, low_ref):
+    solved = lax.dot_general(
+        rows_ref[...], inverse_ref[...], NT, precision=EXACT, preferred_element_type=jnp.float32
+    )
+    low_ref[...] = solved.astype(jnp.bfloat16)
+
+
+def solve_near(inverse, rows):
+    vmem = pl.BlockSpec(memory_space=pltpu.VMEM)
+    return pl.pallas_call(
+        near_kernel,
+        out_shape=jax.ShapeDtypeStruct(rows.shape, jnp.bfloat16),
+        in_specs=[vmem, vmem],
+        out_specs=vmem,
+        cost_estimate=pl.CostEstimate(flops=200_000_000, bytes_accessed=6 * rows.size, transcendentals=0),
+        compiler_params=pltpu.CompilerParams(vmem_limit_bytes=2 << 20),
+        name="solve_near",
+    )(inverse, rows)
+
+
+def solve_panel(diag_block, panel, opened, devices, before):
     vmem, hbm = pl.BlockSpec(memory_space=pltpu.VMEM), pl.BlockSpec(memory_space=pl.ANY)
     panel_hbm = pltpu.with_memory_space_constraint(panel, pltpu.HBM)
-    if before:
-        operands, in_specs = (panel_hbm, diag_block, *before), [hbm, vmem, vmem, vmem]
-    else:
-        operands = (pltpu.with_memory_space_constraint(diag_block, pltpu.HBM), panel_hbm)
-        in_specs = [hbm, hbm]
     return pl.pallas_call(
-        functools.partial(rest_kernel if before else first_kernel, devices),
+        functools.partial(panel_kernel, devices, not before),
         out_shape=(
+            jax.ShapeDtypeStruct(diag_block.shape, jnp.float32),
             jax.ShapeDtypeStruct(panel.shape, jnp.float32),
             jax.ShapeDtypeStruct(panel.shape, jnp.bfloat16),
         ),
-        in_specs=in_specs,
-        out_specs=(vmem, vmem),
-        scratch_shapes=([] if before else [pltpu.VMEM(diag_block.shape, jnp.float32)])
-        + [
-            pltpu.VMEM(panel.shape, jnp.float32),
-            pltpu.VMEM(diag_block.shape, jnp.float32),
-            pltpu.SemaphoreType.DMA((2,)),
-        ],
-        input_output_aliases={2: 0, 3: 1} if before else {},
+        in_specs=[hbm, vmem, vmem] + [vmem] * len(before),
+        out_specs=(vmem, vmem, vmem),
+        scratch_shapes=[pltpu.VMEM(panel.shape, jnp.float32), pltpu.SemaphoreType.DMA],
+        input_output_aliases={3: 0, 4: 1, 5: 2} if before else {},
         cost_estimate=pl.CostEstimate(flops=2_000_000_000, bytes_accessed=8 * panel.size, transcendentals=0),
         compiler_params=pltpu.CompilerParams(vmem_limit_bytes=2 << 20),
         name="solve_rest" if before else "solve_first",
-    )(*operands)
+    )(panel_hbm, diag_block, opened, *before)
 
 
 class Plan:
@@ -184,9 +200,7 @@
                         first.append(k)
             first.sort(reverse=True)
             rest = [k for k in range(pcols - 2, 0, -2) if k not in first]
-            if self.far and not first:
-                first, rest = rest[-1:], rest[:-1]
-            self.flips.append([0] + first + rest)
+            self.flips.append([0] + sorted(first + rest, key=lambda k: k != 2))
         self.places = [[None] * (prows * pcols) for _ in range(self.strips_each)]
         for row in range(prows):
             for me in range(pcols):
@@ -305,14 +319,19 @@
     device = row * pcols + me
     both = ("prow", "pcol")
     partner = [(i, i ^ 1) for i in range(pcols)]
-    own, low = solve_panel(diag_block, panel, plan.sources, ())
+    opened = mark()
+    opened = mark(opened)
+    arrived = []
+    if plan.slots > 1:
+        arrived.append(lax.ppermute(panel, both, plan.pairs(1)))
+    inverse, own, low = solve_panel(diag_block, panel, opened, plan.sources, ())
     if plan.far:
         at = plan.far[0][2]
         far = lax.ppermute(low[at : at + plan.step], both, plan.far_pairs())
-        own, low = solve_panel(diag_block, panel, plan.sources, (own, low))
-    solved = [low]
-    for j in range(1, plan.slots):
-        solved.append(lax.ppermute(low, both, plan.pairs(j)))
+        inverse, own, low = solve_panel(diag_block, panel, opened, plan.sources, (inverse, own, low))
+    for j in range(2, plan.slots):
+        arrived.append(lax.ppermute(low, both, plan.pairs(j)))
+    solved = [low, *(solve_near(inverse, rows) for rows in arrived[:1]), *arrived[1:]]
 
     strips = []
     for places in plan.places:

time: 24.3 us -> 21.9 us (0.901)
  waiting for transfers between devices: 5.09 us -> 4.04 us
  Pallas kernels: 6.29 us -> 5.67 us
  starting transfers between devices: 11.9 us -> 11.3 us
    ppermute x1, starting transfers between devices: 4.48 us -> 1.63 us  [per_device(): far = lax.ppermute(low[at:at + plan.step], both, plan.far_pairs())]
    ppermute x3, starting transfers between devices: 3.11 us -> 5.43 us  [the longest x1 3.12 us: per_device(): arrived.append(lax.ppermute(panel, both, plan.pairs(1)))]
    ppermute x1, waiting for transfers between devices: 1.56 us -> 0.01 us  [per_device(): far = lax.ppermute(low[at:at + plan.step], both, plan.far_pairs())]
    ppermute x3, waiting for transfers between devices: 1.02 us -> 2.18 us  [the longest x2 2.18 us: per_device(): arrived.append(lax.ppermute(low, both, plan.pairs(j)))]
    ppermute x3, waiting for transfers between devices: 2.5 us -> 1.83 us  [per_device(): lax.ppermute(passed, 'prow', [(i, i ^ k) for i in range(prows)])]
    pallas_call x2 -> x5, Pallas kernels: 3.81 us -> 3.18 us  [the longest x2 2.9 us: solve_panel(): pl.pallas_call(functools.partial(panel_kernel, devices, not before), out_...]
  transfers between devices with their start and end apart: 12 -> 12, of which waited for: 4 -> 2; matrix products, arithmetic and copies ran while one was open for 0% -> 0% of each run, Pallas kernels for 5% -> 20%
where the time goes in v4:
time: 21.9 us; the launch traced here: 21.8 us
  starting transfers between devices  11.3 us (52%)
  Pallas kernels  5.67 us (26%)
  waiting for transfers between devices  4.04 us (18%)
  between operations  0.78 us (4%)
    ppermute x3, starting transfers between devices, per_device(): lax.ppermute(passed, 'prow', [(i, i ^ k) for i in range(prows)])  3.55 us
    ppermute x1, starting transfers between devices, per_device(): arrived.append(lax.ppermute(panel, both, plan.pairs(1)))  3.12 us
    pallas_call x2, Pallas kernels, solve_panel(): pl.pallas_call(functools.partial(panel_kernel, devices, not before), out_...  2.9 us
    pallas_call x2, Pallas kernels, update(): pl.pallas_call(functools.partial(update_kernel, plan, len(solved), sides,...  2.48 us
    ppermute x2, starting transfers between devices, per_device(): arrived.append(lax.ppermute(low, both, plan.pairs(j)))  2.32 us
    ppermute x2, waiting for transfers between devices, per_device(): arrived.append(lax.ppermute(low, both, plan.pairs(j)))  2.18 us
    ppermute x3, waiting for transfers between devices, per_device(): lax.ppermute(passed, 'prow', [(i, i ^ k) for i in range(prows)])  1.83 us
    ppermute x1, starting transfers between devices, per_device(): far = lax.ppermute(low[at:at + plan.step], both, plan.far_pairs())  1.63 us
  transfers between devices with their start and end apart: 12, of which 2 were waited for; matrix products, arithmetic and copies ran while one was open for 0% of the time, Pallas kernels for 20%

profile of v4, /device:TPU:0, one launch (start us, length us, event | category | flops | bytes accessed | tf_op | source)
XLA Modules:
  0.0 21.8 jit_solution(17855348149450267272)
XLA Ops:
  0.6 0.0 copy-start.1
  0.6 3.1 %collective-permute-start = (f32[256,128]{1,0:T(8,128)}, f32[256,128]{1,0:T(8,128)S(1)}, u32[]{:S(2)}, u32[]{:S(2)}) collective-permute-start(f32[256,128]{1,0:T(8,128)} %panel_hbm.3), channel_id=1, source_target_pairs={{0,2},{1,3},{2,0},{3,1},{4,6},{5,7},{6,4},{7,5},{8,10},{9,11},{10,... | collective-permute-start | bytes 393224 | tf_op jit(solution)/shard_map/ppermute | solution.py:326
  3.8 0.0 copy-done.1
  3.8 2.9 %solve_first.1 = (f32[128,128]{1,0:T(8,128)S(1)}, f32[256,128]{1,0:T(8,128)S(1)}, bf16[256,128]{1,0:T(8,128)(2,1)S(1)}) custom-call(f32[256,128]{1,0:T(8,128)} %panel_hbm.3, f32[128,128]{1,0:T(8,128)S(1)} %copy-done.1, f32[8,128]{1,0:T(8,128)S(1)} %mark.3._), custom_call_target="tpu_custom_call" | custom-call | flops 2000000000 | bytes 262144 | tf_op jit(solution)/shard_map/solve_first/pallas_call | solution.py:142
  6.7 1.6 %collective-permute-start.7 = (bf16[128,128]{1,0:T(8,128)(2,1)S(1)}, bf16[128,128]{1,0:T(8,128)(2,1)S(1)}, u32[]{:S(2)}, u32[]{:S(2)}) collective-permute-start(bf16[128,128]{1,0:T(8,128)(2,1)S(1)} %slice.10), channel_id=1, source_target_pairs={{0,4},{1,5},{8,12},{9,13},{16,22},{17,23},{24,30},{25,31}} | collective-permute-start | bytes 98312 | tf_op jit(solution)/shard_map/ppermute | solution.py:330
  8.3 0.0 copy-start
  8.3 2.3 %collective-permute-start.2 = (bf16[256,128]{1,0:T(8,128)(2,1)S(1)}, bf16[256,128]{1,0:T(8,128)(2,1)S(1)}, u32[]{:S(2)}, u32[]{:S(2)}) collective-permute-start(bf16[256,128]{1,0:T(8,128)(2,1)S(1)} %get-tuple-element.13.refs_0_), channel_id=1, source_target_pairs={{0,4},{1,5},{2,6},{3,7},{4,0},{5,1},{6,2},{7,3},{8,12},{9,13},{10,... | collective-permute-start | bytes 196616 | tf_op jit(solution)/shard_map/ppermute | solution.py:333
  10.7 0.0 collective-permute-start.1
  10.7 0.0 collective-permute-done.rows_ref
  10.7 0.3 %solve_near.1.refs_1_ = bf16[256,128]{1,0:T(8,128)(2,1)S(1)} custom-call(f32[128,128]{1,0:T(8,128)S(1)} %get-tuple-element.14.inverse_ref, f32[256,128]{1,0:T(8,128)S(1)} %collective-permute-done.rows_ref), custom_call_target="tpu_custom_call" | custom-call | flops 200000000 | bytes 196608 | tf_op jit(solution)/shard_map/solve_near/pallas_call | solution.py:128
  10.9 0.0 collective-permute-done.7
  11.0 1.6 %collective-permute-start.10 = (bf16[128,128]{1,0:T(8,128)(2,1)S(1)}, bf16[128,128]{1,0:T(8,128)(2,1)S(1)}, u32[]{:S(2)}, u32[]{:S(2)}) collective-permute-start(bf16[128,128]{1,0:T(8,128)(2,1)S(1)} %slice_select_fusion), channel_id=1, source_target_pairs={{0,8},{8,0},{16,24},{24,16},{1,9},{9,1},{17,25},{25,17},{2,10},{10... | collective-permute-start | bytes 98312 | tf_op jit(solution)/shard_map/ppermute | solution.py:351
  12.5 1.8 %collective-permute-start.9 = (bf16[128,128]{1,0:T(8,128)(2,1)S(1)}, bf16[128,128]{1,0:T(8,128)(2,1)S(1)}, u32[]{:S(2)}, u32[]{:S(2)}) collective-permute-start(bf16[128,128]{1,0:T(8,128)(2,1)S(1)} %slice_select_fusion), channel_id=1, source_target_pairs={{0,16},{8,24},{16,0},{24,8},{1,17},{9,25},{17,1},{25,9},{2,18},{10... | collective-permute-start | bytes 98312 | tf_op jit(solution)/shard_map/ppermute | solution.py:351
  14.3 0.2 collective-permute-start.8
  14.5 0.0 collective-permute-done.2.refs_3_
  14.5 0.0 collective-permute-start.3
  14.5 2.2 %collective-permute-done.1.refs_2_ = bf16[256,128]{1,0:T(8,128)(2,1)S(1)} collective-permute-done((bf16[256,128]{1,0:T(8,128)(2,1)S(1)}, bf16[256,128]{1,0:T(8,128)(2,1)S(1)}, u32[]{:S(2)}, u32[]{:S(2)}) %collective-permute-start.1) | collective-permute-done | bytes 65568 | tf_op jit(solution)/shard_map/ppermute | solution.py:333
  16.7 0.0 collective-permute-start.6
  16.7 0.0 collective-permute-done.10
  16.7 0.5 %collective-permute-start.5 = (bf16[256,128]{1,0:T(8,128)(2,1)S(1)}, bf16[256,128]{1,0:T(8,128)(2,1)S(1)}, u32[]{:S(2)}, u32[]{:S(2)}) collective-permute-start(bf16[256,128]{1,0:T(8,128)(2,1)S(1)} %collective-permute-done.1.refs_2_), channel_id=1, source_target_pairs={{0,1},{1,0},{2,3},{3,2},{4,5},{5,4},{6,7},{7,6},{8,9},{9,8},{10,11... | collective-permute-start | bytes 196616 | tf_op jit(solution)/shard_map/ppermute | solution.py:353
  17.2 0.0 collective-permute-done.9
  17.2 0.1 collective-permute-start.4
  17.3 1.8 %collective-permute-done.8 = bf16[128,128]{1,0:T(8,128)(2,1)S(1)} collective-permute-done((bf16[128,128]{1,0:T(8,128)(2,1)S(1)}, bf16[128,128]{1,0:T(8,128)(2,1)S(1)}, u32[]{:S(2)}, u32[]{:S(2)}) %collective-permute-start.8) | collective-permute-done | bytes 32800 | tf_op jit(solution)/shard_map/ppermute | solution.py:351
  19.2 0.1 collective-permute-start.11
  19.2 0.0 collective-permute-done.3.refs_4_
  19.2 0.0 collective-permute-done.6.refs_7_
  19.3 0.0 collective-permute-done.5.refs_6_
  19.3 0.0 collective-permute-done.4.refs_5_
  19.3 0.0 copy-done
  19.3 1.2 %update.1 = (f32[2048,256]{1,0:T(8,128)}, f32[256,128]{1,0:T(8,128)}) custom-call(bf16[256,128]{1,0:T(8,128)(2,1)S(1)} %get-tuple-element.13.refs_0_, bf16[256,128]{1,0:T(8,128)(2,1)S(1)} %solve_near.1.refs_1_, bf16[256,128]{1,0:T(8,128)(2,1)S(1)} %collective-permute-done.1.refs_2_, bf16[256,128]{1,0:T(8,128)(2,1)S(1)} %collective-permute-done.2.refs_3_, ...), custom_call_target="tpu_custom_call" | custom-call | flops 300000000 | bytes 4194304 | tf_op jit(solution)/shard_map/update/pallas_call | solution.py:286
  20.5 0.0 collective-permute-done.11.refs_8_
  20.6 1.2 %update_rest.1 = f32[2048,256]{1,0:T(8,128)} custom-call(bf16[256,128]{1,0:T(8,128)(2,1)S(1)} %get-tuple-element.13.refs_0_, bf16[256,128]{1,0:T(8,128)(2,1)S(1)} %solve_near.1.refs_1_, bf16[256,128]{1,0:T(8,128)(2,1)S(1)} %collective-permute-done.1.refs_2_, bf16[256,128]{1,0:T(8,128)(2,1)S(1)} %collective-permute-done.2.refs_3_, ...), custom_call_target="tpu_custom_call", output_to_operand_aliasing={{}: (10, {})} | custom-call | flops 300000000 | bytes 4194304 | tf_op jit(solution)/shard_map/update_rest/pallas_call | solution.py:286
  (6 shorter events, 0.1 us)
Async XLA Ops:
  0.6 3.1 %copy-start.1 = (f32[128,128]{1,0:T(8,128)S(1)}, f32[128,128]{1,0:T(8,128)}, u32[]{:S(2)}) copy-start(f32[128,128]{1,0:T(8,128)} %diag_ref.3) | copy-start | bytes 196612
  0.6 10.0 %collective-permute-start = (f32[256,128]{1,0:T(8,128)}, f32[256,128]{1,0:T(8,128)S(1)}, u32[]{:S(2)}, u32[]{:S(2)}) collective-permute-start(f32[256,128]{1,0:T(8,128)} %panel_hbm.3), channel_id=1, source_target_pairs={{0,2},{1,3},{2,0},{3,1},{4,6},{5,7},{6,4},{7,5},{8,10},{9,11},{10,... | collective-permute-start | bytes 393224 | tf_op jit(solution)/shard_map/ppermute | solution.py:326
  6.7 4.3 %collective-permute-start.7 = (bf16[128,128]{1,0:T(8,128)(2,1)S(1)}, bf16[128,128]{1,0:T(8,128)(2,1)S(1)}, u32[]{:S(2)}, u32[]{:S(2)}) collective-permute-start(bf16[128,128]{1,0:T(8,128)(2,1)S(1)} %slice.10), channel_id=1, source_target_pairs={{0,4},{1,5},{8,12},{9,13},{16,22},{17,23},{24,30},{25,31}} | collective-permute-start | bytes 98312 | tf_op jit(solution)/shard_map/ppermute | solution.py:330
  8.3 11.0 %copy-start = (f32[2048,256]{1,0:T(8,128)S(1)}, f32[2048,256]{1,0:T(8,128)}, u32[]{:S(2)}) copy-start(f32[2048,256]{1,0:T(8,128)} %refs_9_.3) | copy-start | bytes 6291460
  8.3 6.2 %collective-permute-start.2 = (bf16[256,128]{1,0:T(8,128)(2,1)S(1)}, bf16[256,128]{1,0:T(8,128)(2,1)S(1)}, u32[]{:S(2)}, u32[]{:S(2)}) collective-permute-start(bf16[256,128]{1,0:T(8,128)(2,1)S(1)} %get-tuple-element.13.refs_0_), channel_id=1, source_target_pairs={{0,4},{1,5},{2,6},{3,7},{4,0},{5,1},{6,2},{7,3},{8,12},{9,13},{10,... | collective-permute-start | bytes 196616 | tf_op jit(solution)/shard_map/ppermute | solution.py:333
  10.7 6.1 %collective-permute-start.1 = (bf16[256,128]{1,0:T(8,128)(2,1)S(1)}, bf16[256,128]{1,0:T(8,128)(2,1)S(1)}, u32[]{:S(2)}, u32[]{:S(2)}) collective-permute-start(bf16[256,128]{1,0:T(8,128)(2,1)S(1)} %get-tuple-element.13.refs_0_), channel_id=1, source_target_pairs={{0,6},{1,7},{2,4},{3,5},{4,2},{5,3},{6,0},{7,1},{8,14},{9,15},{10,... | collective-permute-start | bytes 196616 | tf_op jit(solution)/shard_map/ppermute | solution.py:333
  11.0 5.7 %collective-permute-start.10 = (bf16[128,128]{1,0:T(8,128)(2,1)S(1)}, bf16[128,128]{1,0:T(8,128)(2,1)S(1)}, u32[]{:S(2)}, u32[]{:S(2)}) collective-permute-start(bf16[128,128]{1,0:T(8,128)(2,1)S(1)} %slice_select_fusion), channel_id=1, source_target_pairs={{0,8},{8,0},{16,24},{24,16},{1,9},{9,1},{17,25},{25,17},{2,10},{10... | collective-permute-start | bytes 98312 | tf_op jit(solution)/shard_map/ppermute | solution.py:351
  12.5 4.7 %collective-permute-start.9 = (bf16[128,128]{1,0:T(8,128)(2,1)S(1)}, bf16[128,128]{1,0:T(8,128)(2,1)S(1)}, u32[]{:S(2)}, u32[]{:S(2)}) collective-permute-start(bf16[128,128]{1,0:T(8,128)(2,1)S(1)} %slice_select_fusion), channel_id=1, source_target_pairs={{0,16},{8,24},{16,0},{24,8},{1,17},{9,25},{17,1},{25,9},{2,18},{10... | collective-permute-start | bytes 98312 | tf_op jit(solution)/shard_map/ppermute | solution.py:351
  14.3 4.8 %collective-permute-start.8 = (bf16[128,128]{1,0:T(8,128)(2,1)S(1)}, bf16[128,128]{1,0:T(8,128)(2,1)S(1)}, u32[]{:S(2)}, u32[]{:S(2)}) collective-permute-start(bf16[128,128]{1,0:T(8,128)(2,1)S(1)} %slice_select_fusion), channel_id=1, source_target_pairs={{0,24},{8,16},{16,8},{24,0},{1,25},{9,17},{17,9},{25,1},{2,26},{10... | collective-permute-start | bytes 98312 | tf_op jit(solution)/shard_map/ppermute | solution.py:351
  14.5 4.7 %collective-permute-start.3 = (bf16[256,128]{1,0:T(8,128)(2,1)S(1)}, bf16[256,128]{1,0:T(8,128)(2,1)S(1)}, u32[]{:S(2)}, u32[]{:S(2)}) collective-permute-start(bf16[256,128]{1,0:T(8,128)(2,1)S(1)} %get-tuple-element.13.refs_0_), channel_id=1, source_target_pairs={{0,1},{1,0},{2,3},{3,2},{4,5},{5,4},{6,7},{7,6},{8,9},{9,8},{10,11... | collective-permute-start | bytes 196616 | tf_op jit(solution)/shard_map/ppermute | solution.py:353
  16.7 2.5 %collective-permute-start.6 = (bf16[256,128]{1,0:T(8,128)(2,1)S(1)}, bf16[256,128]{1,0:T(8,128)(2,1)S(1)}, u32[]{:S(2)}, u32[]{:S(2)}) collective-permute-start(bf16[256,128]{1,0:T(8,128)(2,1)S(1)} %collective-permute-done.2.refs_3_), channel_id=1, source_target_pairs={{0,1},{1,0},{2,3},{3,2},{4,5},{5,4},{6,7},{7,6},{8,9},{9,8},{10,11... | collective-permute-start | bytes 196616 | tf_op jit(solution)/shard_map/ppermute | solution.py:353
  16.7 2.5 %collective-permute-start.5 = (bf16[256,128]{1,0:T(8,128)(2,1)S(1)}, bf16[256,128]{1,0:T(8,128)(2,1)S(1)}, u32[]{:S(2)}, u32[]{:S(2)}) collective-permute-start(bf16[256,128]{1,0:T(8,128)(2,1)S(1)} %collective-permute-done.1.refs_2_), channel_id=1, source_target_pairs={{0,1},{1,0},{2,3},{3,2},{4,5},{5,4},{6,7},{7,6},{8,9},{9,8},{10,11... | collective-permute-start | bytes 196616 | tf_op jit(solution)/shard_map/ppermute | solution.py:353
  17.2 2.0 %collective-permute-start.4 = (bf16[256,128]{1,0:T(8,128)(2,1)S(1)}, bf16[256,128]{1,0:T(8,128)(2,1)S(1)}, u32[]{:S(2)}, u32[]{:S(2)}) collective-permute-start(bf16[256,128]{1,0:T(8,128)(2,1)S(1)} %solve_near.1.refs_1_), channel_id=1, source_target_pairs={{0,1},{1,0},{2,3},{3,2},{4,5},{5,4},{6,7},{7,6},{8,9},{9,8},{10,11... | collective-permute-start | bytes 196616 | tf_op jit(solution)/shard_map/ppermute | solution.py:353
  19.2 1.4 %collective-permute-start.11 = (bf16[128,128]{1,0:T(8,128)(2,1)S(1)}, bf16[128,128]{1,0:T(8,128)(2,1)S(1)}, u32[]{:S(2)}, u32[]{:S(2)}) collective-permute-start(bf16[128,128]{1,0:T(8,128)(2,1)S(1)} %get-tuple-element.19), channel_id=1, source_target_pairs={{0,1},{1,0},{2,3},{3,2},{4,5},{5,4},{6,7},{7,6},{8,9},{9,8},{10,11... | collective-permute-start | bytes 98312 | tf_op jit(solution)/shard_map/ppermute | solution.py:355

commit v5 on v4

--- a/solution.py
+++ b/solution.py
@@ -200,7 +200,7 @@
                         first.append(k)
             first.sort(reverse=True)
             rest = [k for k in range(pcols - 2, 0, -2) if k not in first]
-            self.flips.append([0] + sorted(first + rest, key=lambda k: k != 2))
+            self.flips.append([0] + sorted(first + rest, key=lambda k: (k != 2, k)))
         self.places = [[None] * (prows * pcols) for _ in range(self.strips_each)]
         for row in range(prows):
             for me in range(pcols):
@@ -236,45 +236,49 @@
     return chosen
 
 
-def update_kernel(plan, count, sides, aliased, *refs):
-    x_refs, refs = refs[:count], refs[count:]
+def update_kernel(plan, slots, sides, jobs, aliased, *refs):
+    x_refs, refs = refs[: len(slots)], refs[len(slots) :]
     strip_refs, refs = refs[: len(sides)], refs[len(sides) :]
+    copies = []
     if aliased:
         slab_ref, _, next_ref, column, out_vmem, sems = refs
     else:
         slab_ref, solved_ref, next_ref, factored_ref, column, out_vmem, sems = refs
-        factored_copy = pltpu.make_async_copy(solved_ref, factored_ref, sems.at[count])
-        factored_copy.start()
+        copies.append(pltpu.make_async_copy(solved_ref, factored_ref, sems.at[0]))
+        copies[0].start()
     row, me = lax.axis_index("prow"), lax.axis_index("pcol")
     parity = lax.rem(me, 2)
     step = plan.step
-    across = pl.ds(0, plan.total)
-    if len(sides) == 1:
-        across = pl.ds(pl.multiple_of((parity ^ sides[0]) * step, step), step)
-        whole = strip_refs[0][...]
-    else:
+    if jobs is None:
         for s in range(plan.strips_each):
             for ref, side in zip(strip_refs, sides):
                 at = pl.multiple_of((2 * s + (parity ^ side)) * step, step)
                 column[pl.ds(at, step), :] = ref[s * step : (s + 1) * step, :]
-        whole = column[...]
+        parts = [(i, column[...], pl.ds(0, plan.total), pl.ds(0, plan.total)) for i in range(len(slots))]
+    else:
+        parts = [
+            (
+                i,
+                strip_refs[c][...],
+                pl.ds(pl.multiple_of((parity ^ sides[c]) * step, step), step),
+                pl.ds(c * step, step),
+            )
+            for i, c in jobs
+        ]
     flips = [pick([f[j] for f in plan.flips], row) for j in range(plan.slots)]
-    copies = []
-    for n, ref in enumerate(x_refs):
-        from_column = me ^ flips[n % plan.slots] ^ (n // plan.slots)
-        at = pl.ds(pl.multiple_of(from_column * plan.height, plan.height), plan.height)
-        product = lax.dot_general(ref[...], whole, NT, preferred_element_type=jnp.float32)
-        out_vmem[at, :] = slab_ref[at, across] - product
-        copy = pltpu.make_async_copy(out_vmem.at[at, :], next_ref.at[at, across], sems.at[n])
+    for n, (i, strip, across, held) in enumerate(parts):
+        slot, side = slots[i]
+        at = pl.ds(pl.multiple_of((me ^ flips[slot] ^ side) * plan.height, plan.height), plan.height)
+        product = lax.dot_general(x_refs[i][...], strip, NT, preferred_element_type=jnp.float32)
+        out_vmem[at, held] = slab_ref[at, across] - product
+        copy = pltpu.make_async_copy(out_vmem.at[at, held], next_ref.at[at, across], sems.at[n + 1])
         copy.start()
         copies.append(copy)
-    if not aliased:
-        copies.append(factored_copy)
     for copy in copies:
         copy.wait()
 
 
-def update(plan, solved, strips, sides, slab, own, previous):
+def update(plan, solved, slots, strips, sides, jobs, slab, own, previous):
     vmem, hbm = pl.BlockSpec(memory_space=pltpu.VMEM), pl.BlockSpec(memory_space=pltpu.HBM)
     aliased = previous is not None
     wide = plan.step * plan.strips_each * len(sides)
@@ -284,14 +288,14 @@
         outs.append(jax.ShapeDtypeStruct(own.shape, jnp.float32))
         out_specs.append(hbm)
     return pl.pallas_call(
-        functools.partial(update_kernel, plan, len(solved), sides, aliased),
+        functools.partial(update_kernel, plan, slots, sides, jobs, aliased),
         out_shape=tuple(outs),
         in_specs=[vmem] * (len(operands) - 1) + [hbm if aliased else vmem],
         out_specs=tuple(out_specs),
         scratch_shapes=[
             pltpu.VMEM((plan.total, own.shape[1]), jnp.bfloat16),
             pltpu.VMEM((slab.shape[0], wide), jnp.float32),
-            pltpu.SemaphoreType.DMA((plan.pcols + 1,)),
+            pltpu.SemaphoreType.DMA((len(jobs or solved) + 1,)),
         ],
         input_output_aliases={len(operands) - 1: 0} if aliased else {},
         cost_estimate=pl.CostEstimate(flops=300_000_000, bytes_accessed=8 * slab.size, transcendentals=0),
@@ -353,11 +357,16 @@
         solved.append(lax.ppermute(solved[j], "pcol", partner))
     mine = choose(received, row ^ lax.rem(me, prows))
     other = lax.ppermute(choose(received, row ^ lax.rem(me ^ 1, prows)), "pcol", partner)
+    slots = [(n % plan.slots, n // plan.slots) for n in range(len(solved))]
     if plan.strips_each == 1 and plan.step % LANES == 0:
-        slab_next, factored = update(plan, solved, [mine], (0,), slab, own, None)
-        (slab_next,) = update(plan, solved, [other], (1,), slab, own, slab_next)
+        last = len(solved) - 1
+        slab_next, factored = update(
+            plan, solved[:last], slots[:last], [mine], (0,), [(i, 0) for i in range(last)], slab, own, None
+        )
+        jobs = [(i, 0) for i in range(last + 1)] + [(last, 1)]
+        (slab_next,) = update(plan, solved, slots, [other, mine], (1, 0), jobs, slab, own, slab_next)
     else:
-        slab_next, factored = update(plan, solved, [mine, other], (0, 1), slab, own, None)
+        slab_next, factored = update(plan, solved, slots, [mine, other], (0, 1), None, slab, own, None)
     return slab_next, factored
 
 

time: 21.9 us -> 21.9 us (level)
    ppermute x3, waiting for transfers between devices: 1.83 us -> 1.49 us  [per_device(): lax.ppermute(passed, 'prow', [(i, i ^ k) for i in range(prows)])]
  transfers between devices with their start and end apart: 12 -> 12, of which waited for: 2 -> 3; matrix products, arithmetic and copies ran while one was open for 0% -> 0% of each run, Pallas kernels for 20% -> 20%
where the time goes in v5:
time: 21.9 us; the launch traced here: 21.7 us
  starting transfers between devices  11.3 us (52%)
  Pallas kernels  5.65 us (26%)
  waiting for transfers between devices  3.88 us (18%)
  between operations  0.78 us (4%)
    ppermute x3, starting transfers between devices, per_device(): lax.ppermute(passed, 'prow', [(i, i ^ k) for i in range(prows)])  3.55 us
    ppermute x1, starting transfers between devices, per_device(): arrived.append(lax.ppermute(panel, both, plan.pairs(1)))  3.12 us
    pallas_call x2, Pallas kernels, solve_panel(): pl.pallas_call(functools.partial(panel_kernel, devices, not before), out_...  2.9 us
    pallas_call x2, Pallas kernels, update(): pl.pallas_call(functools.partial(update_kernel, plan, slots, sides, jobs,...  2.47 us
    ppermute x2, starting transfers between devices, per_device(): arrived.append(lax.ppermute(low, both, plan.pairs(j)))  2.39 us
    ppermute x2, waiting for transfers between devices, per_device(): arrived.append(lax.ppermute(low, both, plan.pairs(j)))  2.37 us
    ppermute x1, starting transfers between devices, per_device(): far = lax.ppermute(low[at:at + plan.step], both, plan.far_pairs())  1.63 us
    ppermute x3, waiting for transfers between devices, per_device(): lax.ppermute(passed, 'prow', [(i, i ^ k) for i in range(prows)])  1.49 us
  transfers between devices with their start and end apart: 12, of which 3 were waited for; matrix products, arithmetic and copies ran while one was open for 0% of the time, Pallas kernels for 20%

profile of v5, /device:TPU:0, one launch (start us, length us, event | category | flops | bytes accessed | tf_op | source)
XLA Modules:
  0.0 21.7 jit_solution(16176061978277681443)
XLA Ops:
  0.6 0.0 copy-start.1
  0.6 3.1 %collective-permute-start = (f32[256,128]{1,0:T(8,128)}, f32[256,128]{1,0:T(8,128)S(1)}, u32[]{:S(2)}, u32[]{:S(2)}) collective-permute-start(f32[256,128]{1,0:T(8,128)} %panel_hbm.3), channel_id=1, source_target_pairs={{0,2},{1,3},{2,0},{3,1},{4,6},{5,7},{6,4},{7,5},{8,10},{9,11},{10,... | collective-permute-start | bytes 393224 | tf_op jit(solution)/shard_map/ppermute | solution.py:330
  3.8 0.0 copy-done.1
  3.8 2.9 %solve_first.1 = (f32[128,128]{1,0:T(8,128)S(1)}, f32[256,128]{1,0:T(8,128)S(1)}, bf16[256,128]{1,0:T(8,128)(2,1)S(1)}) custom-call(f32[256,128]{1,0:T(8,128)} %panel_hbm.3, f32[128,128]{1,0:T(8,128)S(1)} %copy-done.1, f32[8,128]{1,0:T(8,128)S(1)} %mark.3._), custom_call_target="tpu_custom_call" | custom-call | flops 2000000000 | bytes 262144 | tf_op jit(solution)/shard_map/solve_first/pallas_call | solution.py:142
  6.7 1.6 %collective-permute-start.7 = (bf16[128,128]{1,0:T(8,128)(2,1)S(1)}, bf16[128,128]{1,0:T(8,128)(2,1)S(1)}, u32[]{:S(2)}, u32[]{:S(2)}) collective-permute-start(bf16[128,128]{1,0:T(8,128)(2,1)S(1)} %slice.10), channel_id=1, source_target_pairs={{0,4},{1,5},{8,12},{9,13},{16,22},{17,23},{24,30},{25,31}} | collective-permute-start | bytes 98312 | tf_op jit(solution)/shard_map/ppermute | solution.py:334
  8.3 0.0 copy-start
  8.3 1.9 %collective-permute-start.2 = (bf16[256,128]{1,0:T(8,128)(2,1)S(1)}, bf16[256,128]{1,0:T(8,128)(2,1)S(1)}, u32[]{:S(2)}, u32[]{:S(2)}) collective-permute-start(bf16[256,128]{1,0:T(8,128)(2,1)S(1)} %get-tuple-element.13.refs_0_), channel_id=1, source_target_pairs={{0,6},{1,7},{2,4},{3,5},{4,2},{5,3},{6,0},{7,1},{8,14},{9,15},{10,... | collective-permute-start | bytes 196616 | tf_op jit(solution)/shard_map/ppermute | solution.py:337
  10.2 0.5 %collective-permute-start.1 = (bf16[256,128]{1,0:T(8,128)(2,1)S(1)}, bf16[256,128]{1,0:T(8,128)(2,1)S(1)}, u32[]{:S(2)}, u32[]{:S(2)}) collective-permute-start(bf16[256,128]{1,0:T(8,128)(2,1)S(1)} %get-tuple-element.13.refs_0_), channel_id=1, source_target_pairs={{0,4},{1,5},{2,6},{3,7},{4,0},{5,1},{6,2},{7,3},{8,12},{9,13},{10,... | collective-permute-start | bytes 196616 | tf_op jit(solution)/shard_map/ppermute | solution.py:337
  10.7 0.0 collective-permute-done.rows_ref
  10.7 0.3 %solve_near.1.refs_1_ = bf16[256,128]{1,0:T(8,128)(2,1)S(1)} custom-call(f32[128,128]{1,0:T(8,128)S(1)} %get-tuple-element.14.inverse_ref, f32[256,128]{1,0:T(8,128)S(1)} %collective-permute-done.rows_ref), custom_call_target="tpu_custom_call" | custom-call | flops 200000000 | bytes 196608 | tf_op jit(solution)/shard_map/solve_near/pallas_call | solution.py:128
  11.0 0.0 collective-permute-done.7
  11.1 1.6 %collective-permute-start.10 = (bf16[128,128]{1,0:T(8,128)(2,1)S(1)}, bf16[128,128]{1,0:T(8,128)(2,1)S(1)}, u32[]{:S(2)}, u32[]{:S(2)}) collective-permute-start(bf16[128,128]{1,0:T(8,128)(2,1)S(1)} %slice_select_fusion), channel_id=1, source_target_pairs={{0,8},{8,0},{16,24},{24,16},{1,9},{9,1},{17,25},{25,17},{2,10},{10... | collective-permute-start | bytes 98312 | tf_op jit(solution)/shard_map/ppermute | solution.py:355
  12.6 1.6 %collective-permute-start.9 = (bf16[128,128]{1,0:T(8,128)(2,1)S(1)}, bf16[128,128]{1,0:T(8,128)(2,1)S(1)}, u32[]{:S(2)}, u32[]{:S(2)}) collective-permute-start(bf16[128,128]{1,0:T(8,128)(2,1)S(1)} %slice_select_fusion), channel_id=1, source_target_pairs={{0,16},{8,24},{16,0},{24,8},{1,17},{9,25},{17,1},{25,9},{2,18},{10... | collective-permute-start | bytes 98312 | tf_op jit(solution)/shard_map/ppermute | solution.py:355
  14.2 0.4 %collective-permute-start.8 = (bf16[128,128]{1,0:T(8,128)(2,1)S(1)}, bf16[128,128]{1,0:T(8,128)(2,1)S(1)}, u32[]{:S(2)}, u32[]{:S(2)}) collective-permute-start(bf16[128,128]{1,0:T(8,128)(2,1)S(1)} %slice_select_fusion), channel_id=1, source_target_pairs={{0,24},{8,16},{16,8},{24,0},{1,25},{9,17},{17,9},{25,1},{2,26},{10... | collective-permute-start | bytes 98312 | tf_op jit(solution)/shard_map/ppermute | solution.py:355
  14.6 0.3 %collective-permute-done.2.refs_3_ = bf16[256,128]{1,0:T(8,128)(2,1)S(1)} collective-permute-done((bf16[256,128]{1,0:T(8,128)(2,1)S(1)}, bf16[256,128]{1,0:T(8,128)(2,1)S(1)}, u32[]{:S(2)}, u32[]{:S(2)}) %collective-permute-start.2) | collective-permute-done | bytes 65568 | tf_op jit(solution)/shard_map/ppermute | solution.py:337
  14.9 0.0 collective-permute-start.3
  14.9 2.1 %collective-permute-done.1.refs_2_ = bf16[256,128]{1,0:T(8,128)(2,1)S(1)} collective-permute-done((bf16[256,128]{1,0:T(8,128)(2,1)S(1)}, bf16[256,128]{1,0:T(8,128)(2,1)S(1)}, u32[]{:S(2)}, u32[]{:S(2)}) %collective-permute-start.1) | collective-permute-done | bytes 65568 | tf_op jit(solution)/shard_map/ppermute | solution.py:337
  17.0 0.0 collective-permute-start.6
  17.0 0.0 collective-permute-done.10
  17.0 0.5 %collective-permute-start.5 = (bf16[256,128]{1,0:T(8,128)(2,1)S(1)}, bf16[256,128]{1,0:T(8,128)(2,1)S(1)}, u32[]{:S(2)}, u32[]{:S(2)}) collective-permute-start(bf16[256,128]{1,0:T(8,128)(2,1)S(1)} %collective-permute-done.1.refs_2_), channel_id=1, source_target_pairs={{0,1},{1,0},{2,3},{3,2},{4,5},{5,4},{6,7},{7,6},{8,9},{9,8},{10,11... | collective-permute-start | bytes 196616 | tf_op jit(solution)/shard_map/ppermute | solution.py:357
  17.5 0.0 collective-permute-done.9
  17.5 0.1 collective-permute-start.4
  17.6 1.5 %collective-permute-done.8 = bf16[128,128]{1,0:T(8,128)(2,1)S(1)} collective-permute-done((bf16[128,128]{1,0:T(8,128)(2,1)S(1)}, bf16[128,128]{1,0:T(8,128)(2,1)S(1)}, u32[]{:S(2)}, u32[]{:S(2)}) %collective-permute-start.8) | collective-permute-done | bytes 32800 | tf_op jit(solution)/shard_map/ppermute | solution.py:355
  19.1 0.1 collective-permute-start.11
  19.2 0.0 collective-permute-done.3.refs_4_
  19.2 0.0 collective-permute-done.5.refs_6_
  19.2 0.0 collective-permute-done.4.refs_5_
  19.2 0.0 copy-done
  19.2 1.2 %update.1 = (f32[2048,256]{1,0:T(8,128)}, f32[256,128]{1,0:T(8,128)}) custom-call(bf16[256,128]{1,0:T(8,128)(2,1)S(1)} %get-tuple-element.13.refs_0_, bf16[256,128]{1,0:T(8,128)(2,1)S(1)} %solve_near.1.refs_1_, bf16[256,128]{1,0:T(8,128)(2,1)S(1)} %collective-permute-done.1.refs_2_, bf16[256,128]{1,0:T(8,128)(2,1)S(1)} %collective-permute-done.2.refs_3_, ...), custom_call_target="tpu_custom_call" | custom-call | flops 300000000 | bytes 4194304 | tf_op jit(solution)/shard_map/update/pallas_call | solution.py:290
  20.4 0.0 collective-permute-done.6.refs_7_
  20.4 0.0 collective-permute-done.11.refs_8_
  20.4 1.3 %update_rest.1 = f32[2048,256]{1,0:T(8,128)} custom-call(bf16[256,128]{1,0:T(8,128)(2,1)S(1)} %get-tuple-element.13.refs_0_, bf16[256,128]{1,0:T(8,128)(2,1)S(1)} %solve_near.1.refs_1_, bf16[256,128]{1,0:T(8,128)(2,1)S(1)} %collective-permute-done.1.refs_2_, bf16[256,128]{1,0:T(8,128)(2,1)S(1)} %collective-permute-done.2.refs_3_, ...), custom_call_target="tpu_custom_call", output_to_operand_aliasing={{}: (11, {})} | custom-call | flops 300000000 | bytes 4194304 | tf_op jit(solution)/shard_map/update_rest/pallas_call | solution.py:290
  (6 shorter events, 0.1 us)
Async XLA Ops:
  0.6 3.1 %copy-start.1 = (f32[128,128]{1,0:T(8,128)S(1)}, f32[128,128]{1,0:T(8,128)}, u32[]{:S(2)}) copy-start(f32[128,128]{1,0:T(8,128)} %diag_ref.3) | copy-start | bytes 196612
  0.6 10.1 %collective-permute-start = (f32[256,128]{1,0:T(8,128)}, f32[256,128]{1,0:T(8,128)S(1)}, u32[]{:S(2)}, u32[]{:S(2)}) collective-permute-start(f32[256,128]{1,0:T(8,128)} %panel_hbm.3), channel_id=1, source_target_pairs={{0,2},{1,3},{2,0},{3,1},{4,6},{5,7},{6,4},{7,5},{8,10},{9,11},{10,... | collective-permute-start | bytes 393224 | tf_op jit(solution)/shard_map/ppermute | solution.py:330
  6.7 4.4 %collective-permute-start.7 = (bf16[128,128]{1,0:T(8,128)(2,1)S(1)}, bf16[128,128]{1,0:T(8,128)(2,1)S(1)}, u32[]{:S(2)}, u32[]{:S(2)}) collective-permute-start(bf16[128,128]{1,0:T(8,128)(2,1)S(1)} %slice.10), channel_id=1, source_target_pairs={{0,4},{1,5},{8,12},{9,13},{16,22},{17,23},{24,30},{25,31}} | collective-permute-start | bytes 98312 | tf_op jit(solution)/shard_map/ppermute | solution.py:334
  8.3 10.9 %copy-start = (f32[2048,256]{1,0:T(8,128)S(1)}, f32[2048,256]{1,0:T(8,128)}, u32[]{:S(2)}) copy-start(f32[2048,256]{1,0:T(8,128)} %refs_10_.1) | copy-start | bytes 6291460
  8.3 6.6 %collective-permute-start.2 = (bf16[256,128]{1,0:T(8,128)(2,1)S(1)}, bf16[256,128]{1,0:T(8,128)(2,1)S(1)}, u32[]{:S(2)}, u32[]{:S(2)}) collective-permute-start(bf16[256,128]{1,0:T(8,128)(2,1)S(1)} %get-tuple-element.13.refs_0_), channel_id=1, source_target_pairs={{0,6},{1,7},{2,4},{3,5},{4,2},{5,3},{6,0},{7,1},{8,14},{9,15},{10,... | collective-permute-start | bytes 196616 | tf_op jit(solution)/shard_map/ppermute | solution.py:337
  10.2 6.8 %collective-permute-start.1 = (bf16[256,128]{1,0:T(8,128)(2,1)S(1)}, bf16[256,128]{1,0:T(8,128)(2,1)S(1)}, u32[]{:S(2)}, u32[]{:S(2)}) collective-permute-start(bf16[256,128]{1,0:T(8,128)(2,1)S(1)} %get-tuple-element.13.refs_0_), channel_id=1, source_target_pairs={{0,4},{1,5},{2,6},{3,7},{4,0},{5,1},{6,2},{7,3},{8,12},{9,13},{10,... | collective-permute-start | bytes 196616 | tf_op jit(solution)/shard_map/ppermute | solution.py:337
  11.1 5.9 %collective-permute-start.10 = (bf16[128,128]{1,0:T(8,128)(2,1)S(1)}, bf16[128,128]{1,0:T(8,128)(2,1)S(1)}, u32[]{:S(2)}, u32[]{:S(2)}) collective-permute-start(bf16[128,128]{1,0:T(8,128)(2,1)S(1)} %slice_select_fusion), channel_id=1, source_target_pairs={{0,8},{8,0},{16,24},{24,16},{1,9},{9,1},{17,25},{25,17},{2,10},{10... | collective-permute-start | bytes 98312 | tf_op jit(solution)/shard_map/ppermute | solution.py:355
  12.6 4.9 %collective-permute-start.9 = (bf16[128,128]{1,0:T(8,128)(2,1)S(1)}, bf16[128,128]{1,0:T(8,128)(2,1)S(1)}, u32[]{:S(2)}, u32[]{:S(2)}) collective-permute-start(bf16[128,128]{1,0:T(8,128)(2,1)S(1)} %slice_select_fusion), channel_id=1, source_target_pairs={{0,16},{8,24},{16,0},{24,8},{1,17},{9,25},{17,1},{25,9},{2,18},{10... | collective-permute-start | bytes 98312 | tf_op jit(solution)/shard_map/ppermute | solution.py:355
  14.2 4.8 %collective-permute-start.8 = (bf16[128,128]{1,0:T(8,128)(2,1)S(1)}, bf16[128,128]{1,0:T(8,128)(2,1)S(1)}, u32[]{:S(2)}, u32[]{:S(2)}) collective-permute-start(bf16[128,128]{1,0:T(8,128)(2,1)S(1)} %slice_select_fusion), channel_id=1, source_target_pairs={{0,24},{8,16},{16,8},{24,0},{1,25},{9,17},{17,9},{25,1},{2,26},{10... | collective-permute-start | bytes 98312 | tf_op jit(solution)/shard_map/ppermute | solution.py:355
  14.9 4.2 %collective-permute-start.3 = (bf16[256,128]{1,0:T(8,128)(2,1)S(1)}, bf16[256,128]{1,0:T(8,128)(2,1)S(1)}, u32[]{:S(2)}, u32[]{:S(2)}) collective-permute-start(bf16[256,128]{1,0:T(8,128)(2,1)S(1)} %get-tuple-element.13.refs_0_), channel_id=1, source_target_pairs={{0,1},{1,0},{2,3},{3,2},{4,5},{5,4},{6,7},{7,6},{8,9},{9,8},{10,11... | collective-permute-start | bytes 196616 | tf_op jit(solution)/shard_map/ppermute | solution.py:357
  17.0 3.4 %collective-permute-start.6 = (bf16[256,128]{1,0:T(8,128)(2,1)S(1)}, bf16[256,128]{1,0:T(8,128)(2,1)S(1)}, u32[]{:S(2)}, u32[]{:S(2)}) collective-permute-start(bf16[256,128]{1,0:T(8,128)(2,1)S(1)} %collective-permute-done.2.refs_3_), channel_id=1, source_target_pairs={{0,1},{1,0},{2,3},{3,2},{4,5},{5,4},{6,7},{7,6},{8,9},{9,8},{10,11... | collective-permute-start | bytes 196616 | tf_op jit(solution)/shard_map/ppermute | solution.py:357
  17.0 2.2 %collective-permute-start.5 = (bf16[256,128]{1,0:T(8,128)(2,1)S(1)}, bf16[256,128]{1,0:T(8,128)(2,1)S(1)}, u32[]{:S(2)}, u32[]{:S(2)}) collective-permute-start(bf16[256,128]{1,0:T(8,128)(2,1)S(1)} %collective-permute-done.1.refs_2_), channel_id=1, source_target_pairs={{0,1},{1,0},{2,3},{3,2},{4,5},{5,4},{6,7},{7,6},{8,9},{9,8},{10,11... | collective-permute-start | bytes 196616 | tf_op jit(solution)/shard_map/ppermute | solution.py:357
  17.5 1.7 %collective-permute-start.4 = (bf16[256,128]{1,0:T(8,128)(2,1)S(1)}, bf16[256,128]{1,0:T(8,128)(2,1)S(1)}, u32[]{:S(2)}, u32[]{:S(2)}) collective-permute-start(bf16[256,128]{1,0:T(8,128)(2,1)S(1)} %solve_near.1.refs_1_), channel_id=1, source_target_pairs={{0,1},{1,0},{2,3},{3,2},{4,5},{5,4},{6,7},{7,6},{8,9},{9,8},{10,11... | collective-permute-start | bytes 196616 | tf_op jit(solution)/shard_map/ppermute | solution.py:357
  19.1 1.3 %collective-permute-start.11 = (bf16[128,128]{1,0:T(8,128)(2,1)S(1)}, bf16[128,128]{1,0:T(8,128)(2,1)S(1)}, u32[]{:S(2)}, u32[]{:S(2)}) collective-permute-start(bf16[128,128]{1,0:T(8,128)(2,1)S(1)} %get-tuple-element.19), channel_id=1, source_target_pairs={{0,1},{1,0},{2,3},{3,2},{4,5},{5,4},{6,7},{7,6},{8,9},{9,8},{10,11... | collective-permute-start | bytes 98312 | tf_op jit(solution)/shard_map/ppermute | solution.py:359

commit v6 on v5

--- a/solution.py
+++ b/solution.py
@@ -116,18 +116,17 @@
     )(*before)
 
 
-def near_kernel(inverse_ref, rows_ref, low_ref):
-    solved = lax.dot_general(
-        rows_ref[...], inverse_ref[...], NT, precision=EXACT, preferred_element_type=jnp.float32
-    )
+def near_kernel(first, inverse_ref, rows_ref, low_ref):
+    rows = rows_ref[first : first + low_ref.shape[0], :]
+    solved = lax.dot_general(rows, inverse_ref[...], NT, precision=EXACT, preferred_element_type=jnp.float32)
     low_ref[...] = solved.astype(jnp.bfloat16)
 
 
-def solve_near(inverse, rows):
+def solve_near(inverse, rows, first, count):
     vmem = pl.BlockSpec(memory_space=pltpu.VMEM)
     return pl.pallas_call(
-        near_kernel,
-        out_shape=jax.ShapeDtypeStruct(rows.shape, jnp.bfloat16),
+        functools.partial(near_kernel, first),
+        out_shape=jax.ShapeDtypeStruct((count, rows.shape[1]), jnp.bfloat16),
         in_specs=[vmem, vmem],
         out_specs=vmem,
         cost_estimate=pl.CostEstimate(flops=200_000_000, bytes_accessed=6 * rows.size, transcendentals=0),
@@ -335,7 +334,14 @@
         inverse, own, low = solve_panel(diag_block, panel, opened, plan.sources, (inverse, own, low))
     for j in range(2, plan.slots):
         arrived.append(lax.ppermute(low, both, plan.pairs(j)))
-    solved = [low, *(solve_near(inverse, rows) for rows in arrived[:1]), *arrived[1:]]
+    solved = [low, *(solve_near(inverse, rows, 0, plan.height) for rows in arrived[:1]), *arrived[1:]]
+
+    def strip_at(slot, at):
+        if slot < 0:
+            return far
+        if slot == 1:
+            return solve_near(inverse, arrived[0], at, plan.step)
+        return solved[slot][at : at + plan.step]
 
     strips = []
     for places in plan.places:
@@ -345,7 +351,7 @@
                 options.setdefault(place, []).append(at)
         strips.append(
             choose(
-                [(far if j < 0 else solved[j][at : at + plan.step], where) for (j, at), where in options.items()],
+                [(strip_at(j, at), where) for (j, at), where in options.items()],
                 device,
             )
         )
@@ -363,7 +369,7 @@
         slab_next, factored = update(
             plan, solved[:last], slots[:last], [mine], (0,), [(i, 0) for i in range(last)], slab, own, None
         )
-        jobs = [(i, 0) for i in range(last + 1)] + [(last, 1)]
+        jobs = [(last, 1), (last, 0)] + [(i, 0) for i in range(last)]
         (slab_next,) = update(plan, solved, slots, [other, mine], (1, 0), jobs, slab, own, slab_next)
     else:
         slab_next, factored = update(plan, solved, slots, [mine, other], (0, 1), None, slab, own, None)

time: 21.9 us -> 21.8 us (level)
  waiting for transfers between devices: 3.88 us -> 3.59 us
  Pallas kernels: 5.65 us -> 5.92 us
    ppermute x2, waiting for transfers between devices: 2.37 us -> 2.1 us  [per_device(): arrived.append(lax.ppermute(low, both, plan.pairs(j)))]
    pallas_call x1 -> x2, Pallas kernels: 0.28 us -> 0.53 us  [solve_near(): pl.pallas_call(functools.partial(near_kernel, first), out_shape=jax.Shape...]
  transfers between devices with their start and end apart: 12 -> 12, of which waited for: 3 -> 3; matrix products, arithmetic and copies ran while one was open for 0% -> 0% of each run, Pallas kernels for 20% -> 21%
where the time goes in v6:
time: 21.8 us; the launch traced here: 21.7 us
  starting transfers between devices  11.4 us (52%)
  Pallas kernels  5.92 us (27%)
  waiting for transfers between devices  3.59 us (16%)
  between operations  0.78 us (4%)
    ppermute x3, starting transfers between devices, per_device(): lax.ppermute(passed, 'prow', [(i, i ^ k) for i in range(prows)])  3.55 us
    ppermute x1, starting transfers between devices, per_device(): arrived.append(lax.ppermute(panel, both, plan.pairs(1)))  3.12 us
    pallas_call x2, Pallas kernels, solve_panel(): pl.pallas_call(functools.partial(panel_kernel, devices, not before), out_...  2.9 us
    pallas_call x2, Pallas kernels, update(): pl.pallas_call(functools.partial(update_kernel, plan, slots, sides, jobs,...  2.48 us
    ppermute x2, starting transfers between devices, per_device(): arrived.append(lax.ppermute(low, both, plan.pairs(j)))  2.39 us
    ppermute x2, waiting for transfers between devices, per_device(): arrived.append(lax.ppermute(low, both, plan.pairs(j)))  2.1 us
    ppermute x1, starting transfers between devices, per_device(): far = lax.ppermute(low[at:at + plan.step], both, plan.far_pairs())  1.63 us
    ppermute x3, waiting for transfers between devices, per_device(): lax.ppermute(passed, 'prow', [(i, i ^ k) for i in range(prows)])  1.46 us
  transfers between devices with their start and end apart: 12, of which 3 were waited for; matrix products, arithmetic and copies ran while one was open for 0% of the time, Pallas kernels for 21%

profile of v6, /device:TPU:0, one launch (start us, length us, event | category | flops | bytes accessed | tf_op | source)
XLA Modules:
  0.0 21.7 jit_solution(9131970883347964055)
XLA Ops:
  0.6 0.0 copy-start.1
  0.6 3.1 %collective-permute-start = (f32[256,128]{1,0:T(8,128)}, f32[256,128]{1,0:T(8,128)S(1)}, u32[]{:S(2)}, u32[]{:S(2)}) collective-permute-start(f32[256,128]{1,0:T(8,128)} %panel_hbm.3), channel_id=1, source_target_pairs={{0,2},{1,3},{2,0},{3,1},{4,6},{5,7},{6,4},{7,5},{8,10},{9,11},{10,... | collective-permute-start | bytes 393224 | tf_op jit(solution)/shard_map/ppermute | solution.py:329
  3.8 0.0 copy-done.1
  3.8 2.9 %solve_first.1 = (f32[128,128]{1,0:T(8,128)S(1)}, f32[256,128]{1,0:T(8,128)S(1)}, bf16[256,128]{1,0:T(8,128)(2,1)S(1)}) custom-call(f32[256,128]{1,0:T(8,128)} %panel_hbm.3, f32[128,128]{1,0:T(8,128)S(1)} %copy-done.1, f32[8,128]{1,0:T(8,128)S(1)} %mark.3._), custom_call_target="tpu_custom_call" | custom-call | flops 2000000000 | bytes 262144 | tf_op jit(solution)/shard_map/solve_first/pallas_call | solution.py:141
  6.7 1.6 %collective-permute-start.7 = (bf16[128,128]{1,0:T(8,128)(2,1)S(1)}, bf16[128,128]{1,0:T(8,128)(2,1)S(1)}, u32[]{:S(2)}, u32[]{:S(2)}) collective-permute-start(bf16[128,128]{1,0:T(8,128)(2,1)S(1)} %slice.6), channel_id=1, source_target_pairs={{0,4},{1,5},{8,12},{9,13},{16,22},{17,23},{24,30},{25,31}} | collective-permute-start | bytes 98312 | tf_op jit(solution)/shard_map/ppermute | solution.py:333
  8.3 0.0 copy-start
  8.3 1.9 %collective-permute-start.2 = (bf16[256,128]{1,0:T(8,128)(2,1)S(1)}, bf16[256,128]{1,0:T(8,128)(2,1)S(1)}, u32[]{:S(2)}, u32[]{:S(2)}) collective-permute-start(bf16[256,128]{1,0:T(8,128)(2,1)S(1)} %get-tuple-element.13.refs_0_), channel_id=1, source_target_pairs={{0,6},{1,7},{2,4},{3,5},{4,2},{5,3},{6,0},{7,1},{8,14},{9,15},{10,... | collective-permute-start | bytes 196616 | tf_op jit(solution)/shard_map/ppermute | solution.py:336
  10.2 0.5 %collective-permute-start.1 = (bf16[256,128]{1,0:T(8,128)(2,1)S(1)}, bf16[256,128]{1,0:T(8,128)(2,1)S(1)}, u32[]{:S(2)}, u32[]{:S(2)}) collective-permute-start(bf16[256,128]{1,0:T(8,128)(2,1)S(1)} %get-tuple-element.13.refs_0_), channel_id=1, source_target_pairs={{0,4},{1,5},{2,6},{3,7},{4,0},{5,1},{6,2},{7,3},{8,12},{9,13},{10,... | collective-permute-start | bytes 196616 | tf_op jit(solution)/shard_map/ppermute | solution.py:336
  10.7 0.0 collective-permute-done.rows_ref
  10.7 0.3 %solve_near.3 = bf16[128,128]{1,0:T(8,128)(2,1)S(1)} custom-call(f32[128,128]{1,0:T(8,128)S(1)} %get-tuple-element.14.inverse_ref, f32[256,128]{1,0:T(8,128)S(1)} %collective-permute-done.rows_ref), custom_call_target="tpu_custom_call" | custom-call | flops 200000000 | bytes 196608 | tf_op jit(solution)/shard_map/solve_near/pallas_call | solution.py:127
  11.0 0.0 collective-permute-done.7
  11.0 1.6 %collective-permute-start.10 = (bf16[128,128]{1,0:T(8,128)(2,1)S(1)}, bf16[128,128]{1,0:T(8,128)(2,1)S(1)}, u32[]{:S(2)}, u32[]{:S(2)}) collective-permute-start(bf16[128,128]{1,0:T(8,128)(2,1)S(1)} %select_select_fusion.2), channel_id=1, source_target_pairs={{0,8},{8,0},{16,24},{24,16},{1,9},{9,1},{17,25},{25,17},{2,10},{10... | collective-permute-start | bytes 98312 | tf_op jit(solution)/shard_map/ppermute | solution.py:361
  12.6 1.6 %collective-permute-start.9 = (bf16[128,128]{1,0:T(8,128)(2,1)S(1)}, bf16[128,128]{1,0:T(8,128)(2,1)S(1)}, u32[]{:S(2)}, u32[]{:S(2)}) collective-permute-start(bf16[128,128]{1,0:T(8,128)(2,1)S(1)} %select_select_fusion.2), channel_id=1, source_target_pairs={{0,16},{8,24},{16,0},{24,8},{1,17},{9,25},{17,1},{25,9},{2,18},{10... | collective-permute-start | bytes 98312 | tf_op jit(solution)/shard_map/ppermute | solution.py:361
  14.2 0.4 %collective-permute-start.8 = (bf16[128,128]{1,0:T(8,128)(2,1)S(1)}, bf16[128,128]{1,0:T(8,128)(2,1)S(1)}, u32[]{:S(2)}, u32[]{:S(2)}) collective-permute-start(bf16[128,128]{1,0:T(8,128)(2,1)S(1)} %select_select_fusion.2), channel_id=1, source_target_pairs={{0,24},{8,16},{16,8},{24,0},{1,25},{9,17},{17,9},{25,1},{2,26},{10... | collective-permute-start | bytes 98312 | tf_op jit(solution)/shard_map/ppermute | solution.py:361
  14.6 0.3 %solve_near.2.refs_1_ = bf16[256,128]{1,0:T(8,128)(2,1)S(1)} custom-call(f32[128,128]{1,0:T(8,128)S(1)} %get-tuple-element.14.inverse_ref, f32[256,128]{1,0:T(8,128)S(1)} %collective-permute-done.rows_ref), custom_call_target="tpu_custom_call" | custom-call | flops 200000000 | bytes 196608 | tf_op jit(solution)/shard_map/solve_near/pallas_call | solution.py:127
  14.9 0.1 collective-permute-done.2.refs_3_
  14.9 0.0 collective-permute-start.3
  15.0 2.0 %collective-permute-done.1.refs_2_ = bf16[256,128]{1,0:T(8,128)(2,1)S(1)} collective-permute-done((bf16[256,128]{1,0:T(8,128)(2,1)S(1)}, bf16[256,128]{1,0:T(8,128)(2,1)S(1)}, u32[]{:S(2)}, u32[]{:S(2)}) %collective-permute-start.1) | collective-permute-done | bytes 65568 | tf_op jit(solution)/shard_map/ppermute | solution.py:336
  17.0 0.0 collective-permute-start.6
  17.0 0.0 collective-permute-done.10
  17.0 0.5 %collective-permute-start.5 = (bf16[256,128]{1,0:T(8,128)(2,1)S(1)}, bf16[256,128]{1,0:T(8,128)(2,1)S(1)}, u32[]{:S(2)}, u32[]{:S(2)}) collective-permute-start(bf16[256,128]{1,0:T(8,128)(2,1)S(1)} %collective-permute-done.1.refs_2_), channel_id=1, source_target_pairs={{0,1},{1,0},{2,3},{3,2},{4,5},{5,4},{6,7},{7,6},{8,9},{9,8},{10,11... | collective-permute-start | bytes 196616 | tf_op jit(solution)/shard_map/ppermute | solution.py:363
  17.5 0.0 collective-permute-done.9
  17.5 0.1 collective-permute-start.4
  17.6 1.5 %collective-permute-done.8 = bf16[128,128]{1,0:T(8,128)(2,1)S(1)} collective-permute-done((bf16[128,128]{1,0:T(8,128)(2,1)S(1)}, bf16[128,128]{1,0:T(8,128)(2,1)S(1)}, u32[]{:S(2)}, u32[]{:S(2)}) %collective-permute-start.8) | collective-permute-done | bytes 32800 | tf_op jit(solution)/shard_map/ppermute | solution.py:361
  19.1 0.1 collective-permute-start.11
  19.1 0.0 collective-permute-done.3.refs_4_
  19.1 0.0 collective-permute-done.5.refs_6_
  19.2 0.0 collective-permute-done.4.refs_5_
  19.2 0.0 copy-done
  19.2 1.2 %update.1 = (f32[2048,256]{1,0:T(8,128)}, f32[256,128]{1,0:T(8,128)}) custom-call(bf16[256,128]{1,0:T(8,128)(2,1)S(1)} %get-tuple-element.13.refs_0_, bf16[256,128]{1,0:T(8,128)(2,1)S(1)} %solve_near.2.refs_1_, bf16[256,128]{1,0:T(8,128)(2,1)S(1)} %collective-permute-done.1.refs_2_, bf16[256,128]{1,0:T(8,128)(2,1)S(1)} %collective-permute-done.2.refs_3_, ...), custom_call_target="tpu_custom_call" | custom-call | flops 300000000 | bytes 4194304 | tf_op jit(solution)/shard_map/update/pallas_call | solution.py:289
  20.4 0.0 collective-permute-done.6.refs_7_
  20.4 0.0 collective-permute-done.11.refs_8_
  20.4 1.3 %update_rest.1 = f32[2048,256]{1,0:T(8,128)} custom-call(bf16[256,128]{1,0:T(8,128)(2,1)S(1)} %get-tuple-element.13.refs_0_, bf16[256,128]{1,0:T(8,128)(2,1)S(1)} %solve_near.2.refs_1_, bf16[256,128]{1,0:T(8,128)(2,1)S(1)} %collective-permute-done.1.refs_2_, bf16[256,128]{1,0:T(8,128)(2,1)S(1)} %collective-permute-done.2.refs_3_, ...), custom_call_target="tpu_custom_call", output_to_operand_aliasing={{}: (11, {})} | custom-call | flops 300000000 | bytes 4194304 | tf_op jit(solution)/shard_map/update_rest/pallas_call | solution.py:289
  (6 shorter events, 0.1 us)
Async XLA Ops:
  0.6 3.1 %copy-start.1 = (f32[128,128]{1,0:T(8,128)S(1)}, f32[128,128]{1,0:T(8,128)}, u32[]{:S(2)}) copy-start(f32[128,128]{1,0:T(8,128)} %diag_ref.3) | copy-start | bytes 196612
  0.6 10.1 %collective-permute-start = (f32[256,128]{1,0:T(8,128)}, f32[256,128]{1,0:T(8,128)S(1)}, u32[]{:S(2)}, u32[]{:S(2)}) collective-permute-start(f32[256,128]{1,0:T(8,128)} %panel_hbm.3), channel_id=1, source_target_pairs={{0,2},{1,3},{2,0},{3,1},{4,6},{5,7},{6,4},{7,5},{8,10},{9,11},{10,... | collective-permute-start | bytes 393224 | tf_op jit(solution)/shard_map/ppermute | solution.py:329
  6.7 4.3 %collective-permute-start.7 = (bf16[128,128]{1,0:T(8,128)(2,1)S(1)}, bf16[128,128]{1,0:T(8,128)(2,1)S(1)}, u32[]{:S(2)}, u32[]{:S(2)}) collective-permute-start(bf16[128,128]{1,0:T(8,128)(2,1)S(1)} %slice.6), channel_id=1, source_target_pairs={{0,4},{1,5},{8,12},{9,13},{16,22},{17,23},{24,30},{25,31}} | collective-permute-start | bytes 98312 | tf_op jit(solution)/shard_map/ppermute | solution.py:333
  8.3 10.9 %copy-start = (f32[2048,256]{1,0:T(8,128)S(1)}, f32[2048,256]{1,0:T(8,128)}, u32[]{:S(2)}) copy-start(f32[2048,256]{1,0:T(8,128)} %refs_10_.1) | copy-start | bytes 6291460
  8.3 6.6 %collective-permute-start.2 = (bf16[256,128]{1,0:T(8,128)(2,1)S(1)}, bf16[256,128]{1,0:T(8,128)(2,1)S(1)}, u32[]{:S(2)}, u32[]{:S(2)}) collective-permute-start(bf16[256,128]{1,0:T(8,128)(2,1)S(1)} %get-tuple-element.13.refs_0_), channel_id=1, source_target_pairs={{0,6},{1,7},{2,4},{3,5},{4,2},{5,3},{6,0},{7,1},{8,14},{9,15},{10,... | collective-permute-start | bytes 196616 | tf_op jit(solution)/shard_map/ppermute | solution.py:336
  10.2 6.8 %collective-permute-start.1 = (bf16[256,128]{1,0:T(8,128)(2,1)S(1)}, bf16[256,128]{1,0:T(8,128)(2,1)S(1)}, u32[]{:S(2)}, u32[]{:S(2)}) collective-permute-start(bf16[256,128]{1,0:T(8,128)(2,1)S(1)} %get-tuple-element.13.refs_0_), channel_id=1, source_target_pairs={{0,4},{1,5},{2,6},{3,7},{4,0},{5,1},{6,2},{7,3},{8,12},{9,13},{10,... | collective-permute-start | bytes 196616 | tf_op jit(solution)/shard_map/ppermute | solution.py:336
  11.0 6.0 %collective-permute-start.10 = (bf16[128,128]{1,0:T(8,128)(2,1)S(1)}, bf16[128,128]{1,0:T(8,128)(2,1)S(1)}, u32[]{:S(2)}, u32[]{:S(2)}) collective-permute-start(bf16[128,128]{1,0:T(8,128)(2,1)S(1)} %select_select_fusion.2), channel_id=1, source_target_pairs={{0,8},{8,0},{16,24},{24,16},{1,9},{9,1},{17,25},{25,17},{2,10},{10... | collective-permute-start | bytes 98312 | tf_op jit(solution)/shard_map/ppermute | solution.py:361
  12.6 4.9 %collective-permute-start.9 = (bf16[128,128]{1,0:T(8,128)(2,1)S(1)}, bf16[128,128]{1,0:T(8,128)(2,1)S(1)}, u32[]{:S(2)}, u32[]{:S(2)}) collective-permute-start(bf16[128,128]{1,0:T(8,128)(2,1)S(1)} %select_select_fusion.2), channel_id=1, source_target_pairs={{0,16},{8,24},{16,0},{24,8},{1,17},{9,25},{17,1},{25,9},{2,18},{10... | collective-permute-start | bytes 98312 | tf_op jit(solution)/shard_map/ppermute | solution.py:361
  14.2 4.8 %collective-permute-start.8 = (bf16[128,128]{1,0:T(8,128)(2,1)S(1)}, bf16[128,128]{1,0:T(8,128)(2,1)S(1)}, u32[]{:S(2)}, u32[]{:S(2)}) collective-permute-start(bf16[128,128]{1,0:T(8,128)(2,1)S(1)} %select_select_fusion.2), channel_id=1, source_target_pairs={{0,24},{8,16},{16,8},{24,0},{1,25},{9,17},{17,9},{25,1},{2,26},{10... | collective-permute-start | bytes 98312 | tf_op jit(solution)/shard_map/ppermute | solution.py:361
  14.9 4.2 %collective-permute-start.3 = (bf16[256,128]{1,0:T(8,128)(2,1)S(1)}, bf16[256,128]{1,0:T(8,128)(2,1)S(1)}, u32[]{:S(2)}, u32[]{:S(2)}) collective-permute-start(bf16[256,128]{1,0:T(8,128)(2,1)S(1)} %get-tuple-element.13.refs_0_), channel_id=1, source_target_pairs={{0,1},{1,0},{2,3},{3,2},{4,5},{5,4},{6,7},{7,6},{8,9},{9,8},{10,11... | collective-permute-start | bytes 196616 | tf_op jit(solution)/shard_map/ppermute | solution.py:363
  17.0 3.4 %collective-permute-start.6 = (bf16[256,128]{1,0:T(8,128)(2,1)S(1)}, bf16[256,128]{1,0:T(8,128)(2,1)S(1)}, u32[]{:S(2)}, u32[]{:S(2)}) collective-permute-start(bf16[256,128]{1,0:T(8,128)(2,1)S(1)} %collective-permute-done.2.refs_3_), channel_id=1, source_target_pairs={{0,1},{1,0},{2,3},{3,2},{4,5},{5,4},{6,7},{7,6},{8,9},{9,8},{10,11... | collective-permute-start | bytes 196616 | tf_op jit(solution)/shard_map/ppermute | solution.py:363
  17.0 2.2 %collective-permute-start.5 = (bf16[256,128]{1,0:T(8,128)(2,1)S(1)}, bf16[256,128]{1,0:T(8,128)(2,1)S(1)}, u32[]{:S(2)}, u32[]{:S(2)}) collective-permute-start(bf16[256,128]{1,0:T(8,128)(2,1)S(1)} %collective-permute-done.1.refs_2_), channel_id=1, source_target_pairs={{0,1},{1,0},{2,3},{3,2},{4,5},{5,4},{6,7},{7,6},{8,9},{9,8},{10,11... | collective-permute-start | bytes 196616 | tf_op jit(solution)/shard_map/ppermute | solution.py:363
  17.5 1.6 %collective-permute-start.4 = (bf16[256,128]{1,0:T(8,128)(2,1)S(1)}, bf16[256,128]{1,0:T(8,128)(2,1)S(1)}, u32[]{:S(2)}, u32[]{:S(2)}) collective-permute-start(bf16[256,128]{1,0:T(8,128)(2,1)S(1)} %solve_near.2.refs_1_), channel_id=1, source_target_pairs={{0,1},{1,0},{2,3},{3,2},{4,5},{5,4},{6,7},{7,6},{8,9},{9,8},{10,11... | collective-permute-start | bytes 196616 | tf_op jit(solution)/shard_map/ppermute | solution.py:363
  19.1 1.3 %collective-permute-start.11 = (bf16[128,128]{1,0:T(8,128)(2,1)S(1)}, bf16[128,128]{1,0:T(8,128)(2,1)S(1)}, u32[]{:S(2)}, u32[]{:S(2)}) collective-permute-start(bf16[128,128]{1,0:T(8,128)(2,1)S(1)} %get-tuple-element.19), channel_id=1, source_target_pairs={{0,1},{1,0},{2,3},{3,2},{4,5},{5,4},{6,7},{7,6},{8,9},{9,8},{10,11... | collective-permute-start | bytes 98312 | tf_op jit(solution)/shard_map/ppermute | solution.py:365
